TPU v7x, 128 devices: a whole 4x4x4 slice. The times are simulated.
128 devices in a mesh: leaf: 128 (over x, y, z, core).
Axes of the slice: x: 4, y: 4, z: 4, core: 2. Of those that a mesh axis runs over, the one named last changes fastest.
Arguments:
- probes: float32 [131072, 1024], P('leaf'), may hold values from -6 to 6
- leaf_basis: float32 [256, 512, 64], P('leaf'), may hold values from -0.25 to 0.25
- leaf_transfer: float32 [256, 64, 64], P('leaf'), may hold values from -0.75 to 0.75
- cluster_transfer: float32 [64, 64, 64], replicated, may hold values from -0.75 to 0.75
- couple_one: float32 [512, 64, 64], P('leaf'), may hold values from -0.75 to 0.75
- pairs_one: int32 [512], P('leaf'), may hold values from 0 to 63, as said below
- count_one: int32 [64], replicated, may hold values from 0 to 8
- couple_two: float32 [128, 64, 64], P('leaf'), may hold values from -0.75 to 0.75
- pairs_two: int32 [128], P('leaf'), may hold values from 0 to 15, as said below
- count_two: int32 [16], replicated, may hold values from 0 to 8
- near_blocks: float32 [256, 3, 512, 512], P('leaf'), may hold values from -0.15625 to 0.15625
- near_list: int32 [256, 3], P('leaf'), may hold values from 0 to 255, as said below
Outputs:
- kernel_times: float32 [131072, 1024], P('leaf')
Inputs may be any that keep to these rules, and one draw needn't show every extreme that they name: `pairs_one`: for slots k < count_one[c], the partners of cluster c are distinct clusters j with |j - c| >= 2 and |j // 4 - c // 4| <= 1; the other slots hold c itself. `pairs_two`: for slots k < count_two[q], the partners of cluster q are distinct clusters j with |j - q| >= 2 and |j // 4 - q // 4| <= 1; the other slots hold q itself. near_list[i, 0] is i, and every entry of row i lies within i - 2 to i + 2.
All inputs are finite; a program needn't handle non-finite values.
Results may differ from a plain program's by a relative error of at most 0.000086.
Values sent between devices are 32-bit elements; how exact they have to be, the bound alone decides.
No kernel may reach another device: no remote copies, remote signals or barrier semaphores. Data moves between devices by JAX's collectives and lax.ppermute only.
A program may use at most 128 MiB of HBM per device.

v0:
```python
import jax
import jax.numpy as jnp
from jax import lax
from jax.sharding import PartitionSpec as P

partner_offsets = (-7, -6, -5, -4, -3, -2, 2, 3, 4, 5, 6, 7)


def swapped(shard, axis, apart):
    return lax.ppermute(shard, axis, [(i, i ^ 1 << apart) for i in range(lax.axis_size(axis))])


def shifted(shard, axis, by):
    peers = lax.axis_size(axis)
    pairs = [(i, i + by) for i in range(peers) if 0 <= i + by < peers]
    return lax.ppermute(shard, axis, pairs)


def padded_2(shard, sides, width):
    for axis, dim in sides:
        peers, length = (lax.axis_size(axis), shard.shape[dim])
        up = [(i, (i + 1) % peers) for i in range(peers - 1)]
        down = [(j, i) for i, j in up]
        last = lax.slice_in_dim(shard, length - width, length, axis=dim)
        leading = lax.slice_in_dim(shard, 0, width, axis=dim)
        before = lax.ppermute(last, axis, up)
        after = lax.ppermute(leading, axis, down)
        shard = jnp.concatenate([before, shard, after], axis=dim)
    return shard


def upward_sum(coeffs, first_bit, last_bit):
    for bit_index in range(first_bit, last_bit):
        coeffs = coeffs + swapped(coeffs, "leaf", bit_index)
    return coeffs


def coupled_sum(totals, last_bit):
    for bit_index in range(last_bit):
        totals = totals + swapped(totals, "leaf", bit_index)
    return totals


def fetch_partners(coeffs, stride, devices):
    usable = [offset for offset in partner_offsets if abs(offset) * stride < devices]
    stacked = jnp.stack([shifted(coeffs, "leaf", -offset * stride) for offset in usable])
    return (stacked, jnp.array(usable, jnp.int32))


def make_picker(stacked, usable):
    highest = lax.Precision.HIGHEST

    def picker(partner_ids, owners):
        select = ((partner_ids - owners)[:, None] == usable[None, :]).astype(jnp.float32)
        return jnp.einsum("ko,orp->krp", select, stacked, precision=highest)

    return picker


def couple_level(coupling, partner_ids, counts, picker, first_slot, slots_each):
    highest = lax.Precision.HIGHEST
    slot_total = partner_ids.shape[0]
    slot_index = first_slot + jnp.arange(slot_total, dtype=jnp.int32)
    owners = slot_index // slots_each
    within = slot_index % slots_each
    valid = (within < jnp.take(counts, owners)).astype(jnp.float32)
    partner = picker(partner_ids, owners) * valid[:, None, None]
    return jnp.einsum("krs,ksp->rp", coupling, partner, precision=highest)


def body(
    probes,
    leaf_basis,
    leaf_transfer,
    cluster_transfer,
    couple_one,
    pairs_one,
    count_one,
    couple_two,
    pairs_two,
    count_two,
    near_blocks,
    near_list,
):
    highest = lax.Precision.HIGHEST
    devices = lax.axis_size("leaf")
    position = lax.axis_index("leaf")
    leaf_count, leaf_size, rank_size = leaf_basis.shape
    width = probes.shape[1]
    blocks = probes.reshape(leaf_count, leaf_size, width)
    leaf_coef = jnp.einsum("lnr,lnp->lrp", leaf_basis, blocks, precision=highest)
    part_one = jnp.einsum("lrs,lrp->sp", leaf_transfer, leaf_coef, precision=highest)
    stride_one = 4 // leaf_count
    stride_two = 16 // leaf_count
    bits_one = stride_one.bit_length() - 1
    bits_two = stride_two.bit_length() - 1
    own_one = position * leaf_count // 4
    own_transfer = lax.dynamic_index_in_dim(cluster_transfer, own_one, 0, keepdims=False)
    slots_one = pairs_one.shape[0]
    slots_two = pairs_two.shape[0]
    slots_each = slots_one * stride_one
    coef_one = upward_sum(part_one, 0, bits_one)
    lifted = jnp.einsum("rs,rp->sp", own_transfer, coef_one, precision=highest)
    coef_two = upward_sum(lifted, bits_one, bits_two)
    stacked_one, usable_one = fetch_partners(coef_one, stride_one, devices)
    stacked_two, usable_two = fetch_partners(coef_two, stride_two, devices)
    picker_one = make_picker(stacked_one, usable_one)
    picker_two = make_picker(stacked_two, usable_two)
    partial_one = couple_level(
        couple_one, pairs_one, count_one, picker_one, position * slots_one, slots_each
    )
    partial_two = couple_level(
        couple_two, pairs_two, count_two, picker_two, position * slots_two, slots_each
    )
    far_one = coupled_sum(partial_one, bits_one)
    far_two = coupled_sum(partial_two, bits_two)
    down_one = far_one + jnp.einsum("rs,sp->rp", own_transfer, far_two, precision=highest)
    child = jnp.einsum("lrs,sp->lrp", leaf_transfer, down_one, precision=highest)
    far_rows = jnp.einsum("lnr,lrp->lnp", leaf_basis, child, precision=highest)
    padded = padded_2(probes, (("leaf", 0),), leaf_count * leaf_size)
    padded = padded.reshape(3 * leaf_count, leaf_size, width)
    local_index = near_list - (position * leaf_count - leaf_count)
    near_rows = jnp.take(padded, local_index.reshape(-1), axis=0).reshape(
        leaf_count, -1, leaf_size, width
    )
    near_part = jnp.einsum("lmab,lmbp->lap", near_blocks, near_rows, precision=highest)
    return (far_rows + near_part).reshape(-1, width)


def solution(mesh):
    return jax.shard_map(
        body,
        mesh=mesh,
        in_specs=(
            P("leaf", None),
            P("leaf", None, None),
            P("leaf", None, None),
            P(),
            P("leaf", None, None),
            P("leaf"),
            P(),
            P("leaf", None, None),
            P("leaf"),
            P(),
            P("leaf", None, None, None),
            P("leaf", None),
        ),
        out_specs=P("leaf", None),
        check_vma=False,
    )
```

profile of v0, /device:TPU:2, one launch (start us, length us, event | category | flops | bytes accessed | tf_op | source)
XLA Modules:
  0.0 283.3 jit_solution(7071995832706483808)
XLA Ops:
  0.0 2.1 collective-permute-start.31
  2.1 7.9 %collective-permute-start.32 = (f32[1024,1024]{1,0:T(8,128)}, f32[1024,1024]{1,0:T(8,128)}, u32[]{:S(2)}, u32[]{:S(2)}) collective-permute-start(f32[1024,1024]{1,0:T(8,128)} %param.14), channel_id=1, source_target_pairs={{1,0},{2,1},{3,2},{4,3},{5,4},{6,5},{7,6},{8,7},{9,8},{10,9},{11,1... | collective-permute-start | bytes 12582920 | tf_op jit(solution)/shard_map/ppermute | solution.py:27
  10.0 4.9 %fusion.37 = f32[2,64,1024]{2,1,0:T(8,128)S(1)} fusion(f32[2,512,64]{1,2,0:T(8,128)} %param.15, f32[2,512,1024]{2,1,0:T(8,128)} %bitcast.109), kind=kOutput, calls=%fused_computation.89 | convolution fusion | flops 805306368 | bytes 4980736 | tf_op jit(solution)/shard_map/lnr,lnp->lrp/dot_general | solution.py:91
  17.0 2.7 collective-permute-start.1
  21.6 5.4 %collective-permute-start.7 = (f32[64,1024]{1,0:T(8,128)S(1)}, f32[64,1024]{1,0:T(8,128)S(1)}, u32[]{:S(2)}, u32[]{:S(2)}) collective-permute-start(f32[64,1024]{1,0:T(8,128)S(1)} %add.135), channel_id=1, source_target_pairs={{4,0},{5,1},{6,2},{7,3},{8,4},{9,5},{10,6},{11,7},{12,8},{13,9},{1... | collective-permute-start | bytes 786440 | tf_op jit(solution)/shard_map/ppermute | solution.py:16
  27.0 3.0 %collective-permute-start.2 = (f32[64,1024]{1,0:T(8,128)S(1)}, f32[64,1024]{1,0:T(8,128)S(1)}, u32[]{:S(2)}, u32[]{:S(2)}) collective-permute-start(f32[64,1024]{1,0:T(8,128)S(1)} %add.135), channel_id=1, source_target_pairs={{0,12},{1,13},{2,14},{3,15},{4,16},{5,17},{6,18},{7,19},{8,20},{9,... | collective-permute-start | bytes 786440 | tf_op jit(solution)/shard_map/ppermute | solution.py:16
  30.4 1.9 collective-permute-done.1
  32.3 2.9 %collective-permute-start.3 = (f32[64,1024]{1,0:T(8,128)S(1)}, f32[64,1024]{1,0:T(8,128)S(1)}, u32[]{:S(2)}, u32[]{:S(2)}) collective-permute-start(f32[64,1024]{1,0:T(8,128)S(1)} %add.135), channel_id=1, source_target_pairs={{0,10},{1,11},{2,12},{3,13},{4,14},{5,15},{6,16},{7,17},{8,18},{9,... | collective-permute-start | bytes 786440 | tf_op jit(solution)/shard_map/ppermute | solution.py:16
  35.3 10.2 %collective-permute-done.2 = f32[64,1024]{1,0:T(8,128)S(1)} collective-permute-done((f32[64,1024]{1,0:T(8,128)S(1)}, f32[64,1024]{1,0:T(8,128)S(1)}, u32[]{:S(2)}, u32[]{:S(2)}) %collective-permute-start.2) | collective-permute-done | bytes 262176 | tf_op jit(solution)/shard_map/ppermute | solution.py:16
  45.5 2.3 collective-permute-start.4
  47.9 9.0 %collective-permute-done.3 = f32[64,1024]{1,0:T(8,128)S(1)} collective-permute-done((f32[64,1024]{1,0:T(8,128)S(1)}, f32[64,1024]{1,0:T(8,128)S(1)}, u32[]{:S(2)}, u32[]{:S(2)}) %collective-permute-start.3) | collective-permute-done | bytes 262176 | tf_op jit(solution)/shard_map/ppermute | solution.py:16
  56.9 1.9 collective-permute-start.5
  58.9 3.0 %collective-permute-start.6 = (f32[64,1024]{1,0:T(8,128)S(1)}, f32[64,1024]{1,0:T(8,128)S(1)}, u32[]{:S(2)}, u32[]{:S(2)}) collective-permute-start(f32[64,1024]{1,0:T(8,128)S(1)} %add.135), channel_id=1, source_target_pairs={{0,4},{1,5},{2,6},{3,7},{4,8},{5,9},{6,10},{7,11},{8,12},{9,13},{1... | collective-permute-start | bytes 786440 | tf_op jit(solution)/shard_map/ppermute | solution.py:16
  61.9 15.6 %collective-permute-done.5 = f32[64,1024]{1,0:T(8,128)S(1)} collective-permute-done((f32[64,1024]{1,0:T(8,128)S(1)}, f32[64,1024]{1,0:T(8,128)S(1)}, u32[]{:S(2)}, u32[]{:S(2)}) %collective-permute-start.5) | collective-permute-done | bytes 262176 | tf_op jit(solution)/shard_map/ppermute | solution.py:16
  77.6 8.0 %collective-permute-start.8 = (f32[64,1024]{1,0:T(8,128)S(1)}, f32[64,1024]{1,0:T(8,128)S(1)}, u32[]{:S(2)}, u32[]{:S(2)}) collective-permute-start(f32[64,1024]{1,0:T(8,128)S(1)} %add.135), channel_id=1, source_target_pairs={{6,0},{7,1},{8,2},{9,3},{10,4},{11,5},{12,6},{13,7},{14,8},{15,9},... | collective-permute-start | bytes 786440 | tf_op jit(solution)/shard_map/ppermute | solution.py:16
  85.7 7.6 %collective-permute-start.9 = (f32[64,1024]{1,0:T(8,128)S(1)}, f32[64,1024]{1,0:T(8,128)S(1)}, u32[]{:S(2)}, u32[]{:S(2)}) collective-permute-start(f32[64,1024]{1,0:T(8,128)S(1)} %add.135), channel_id=1, source_target_pairs={{8,0},{9,1},{10,2},{11,3},{12,4},{13,5},{14,6},{15,7},{16,8},{17,9... | collective-permute-start | bytes 786440 | tf_op jit(solution)/shard_map/ppermute | solution.py:16
  93.4 2.0 collective-permute-start.15
  95.3 7.7 %collective-permute-start.10 = (f32[64,1024]{1,0:T(8,128)S(1)}, f32[64,1024]{1,0:T(8,128)S(1)}, u32[]{:S(2)}, u32[]{:S(2)}) collective-permute-start(f32[64,1024]{1,0:T(8,128)S(1)} %add.135), channel_id=1, source_target_pairs={{10,0},{11,1},{12,2},{13,3},{14,4},{15,5},{16,6},{17,7},{18,8},{19... | collective-permute-start | bytes 786440 | tf_op jit(solution)/shard_map/ppermute | solution.py:16
  103.1 10.7 %collective-permute-start.12 = (f32[64,1024]{1,0:T(8,128)S(1)}, f32[64,1024]{1,0:T(8,128)S(1)}, u32[]{:S(2)}, u32[]{:S(2)}) collective-permute-start(f32[64,1024]{1,0:T(8,128)S(1)} %add.135), channel_id=1, source_target_pairs={{14,0},{15,1},{16,2},{17,3},{18,4},{19,5},{20,6},{21,7},{22,8},{23... | collective-permute-start | bytes 786440 | tf_op jit(solution)/shard_map/ppermute | solution.py:16
  115.2 4.4 %collective-permute-start.17 = (f32[64,1024]{1,0:T(8,128)S(1)}, f32[64,1024]{1,0:T(8,128)S(1)}, u32[]{:S(2)}, u32[]{:S(2)}) collective-permute-start(f32[64,1024]{1,0:T(8,128)S(1)} %add.145), channel_id=1, source_target_pairs={{0,48},{1,49},{2,50},{3,51},{4,52},{5,53},{6,54},{7,55},{8,56},{9,... | collective-permute-start | bytes 786440 | tf_op jit(solution)/shard_map/ppermute | solution.py:16
  119.7 2.6 collective-permute-done.16
  122.3 5.2 %collective-permute-start.18 = (f32[64,1024]{1,0:T(8,128)S(1)}, f32[64,1024]{1,0:T(8,128)S(1)}, u32[]{:S(2)}, u32[]{:S(2)}) collective-permute-start(f32[64,1024]{1,0:T(8,128)S(1)} %add.145), channel_id=1, source_target_pairs={{0,40},{1,41},{2,42},{3,43},{4,44},{5,45},{6,46},{7,47},{8,48},{9,... | collective-permute-start | bytes 786440 | tf_op jit(solution)/shard_map/ppermute | solution.py:16
  127.6 7.5 %collective-permute-start.19 = (f32[64,1024]{1,0:T(8,128)S(1)}, f32[64,1024]{1,0:T(8,128)S(1)}, u32[]{:S(2)}, u32[]{:S(2)}) collective-permute-start(f32[64,1024]{1,0:T(8,128)S(1)} %add.145), channel_id=1, source_target_pairs={{0,32},{1,33},{2,34},{3,35},{4,36},{5,37},{6,38},{7,39},{8,40},{9,... | collective-permute-start | bytes 786440 | tf_op jit(solution)/shard_map/ppermute | solution.py:16
  135.2 7.8 %collective-permute-start.20 = (f32[64,1024]{1,0:T(8,128)S(1)}, f32[64,1024]{1,0:T(8,128)S(1)}, u32[]{:S(2)}, u32[]{:S(2)}) collective-permute-start(f32[64,1024]{1,0:T(8,128)S(1)} %add.145), channel_id=1, source_target_pairs={{0,24},{1,25},{2,26},{3,27},{4,28},{5,29},{6,30},{7,31},{8,32},{9,... | collective-permute-start | bytes 786440 | tf_op jit(solution)/shard_map/ppermute | solution.py:16
  143.0 1.9 collective-permute-start.21
  145.0 2.1 collective-permute-done.20
  147.1 4.2 %collective-permute-start.22 = (f32[64,1024]{1,0:T(8,128)S(1)}, f32[64,1024]{1,0:T(8,128)S(1)}, u32[]{:S(2)}, u32[]{:S(2)}) collective-permute-start(f32[64,1024]{1,0:T(8,128)S(1)} %add.145), channel_id=1, source_target_pairs={{16,0},{17,1},{18,2},{19,3},{20,4},{21,5},{22,6},{23,7},{24,8},{25... | collective-permute-start | bytes 786440 | tf_op jit(solution)/shard_map/ppermute | solution.py:16
  151.4 2.9 %collective-permute-done.21 = f32[64,1024]{1,0:T(8,128)S(1)} collective-permute-done((f32[64,1024]{1,0:T(8,128)S(1)}, f32[64,1024]{1,0:T(8,128)S(1)}, u32[]{:S(2)}, u32[]{:S(2)}) %collective-permute-start.21) | collective-permute-done | bytes 262176 | tf_op jit(solution)/shard_map/ppermute | solution.py:16
  154.3 1.9 collective-permute-start.23
  156.2 2.7 collective-permute-done.22
  158.9 1.9 collective-permute-start.24
  160.9 6.9 %collective-permute-done.23 = f32[64,1024]{1,0:T(8,128)S(1)} collective-permute-done((f32[64,1024]{1,0:T(8,128)S(1)}, f32[64,1024]{1,0:T(8,128)S(1)}, u32[]{:S(2)}, u32[]{:S(2)}) %collective-permute-start.23) | collective-permute-done | bytes 262176 | tf_op jit(solution)/shard_map/ppermute | solution.py:16
  169.1 6.4 %collective-permute-done.24 = f32[64,1024]{1,0:T(8,128)S(1)} collective-permute-done((f32[64,1024]{1,0:T(8,128)S(1)}, f32[64,1024]{1,0:T(8,128)S(1)}, u32[]{:S(2)}, u32[]{:S(2)}) %collective-permute-start.24) | collective-permute-done | bytes 262176 | tf_op jit(solution)/shard_map/ppermute | solution.py:16
  176.8 9.4 %collective-permute-done.25 = f32[64,1024]{1,0:T(8,128)S(1)} collective-permute-done((f32[64,1024]{1,0:T(8,128)S(1)}, f32[64,1024]{1,0:T(8,128)S(1)}, u32[]{:S(2)}, u32[]{:S(2)}) %collective-permute-start.25) | collective-permute-done | bytes 262176 | tf_op jit(solution)/shard_map/ppermute | solution.py:16
  187.5 1.4 collective-permute-done.26
  188.9 1.9 collective-permute-start.11
  190.8 7.1 %collective-permute-done.27 = f32[64,1024]{1,0:T(8,128)S(1)} collective-permute-done((f32[64,1024]{1,0:T(8,128)S(1)}, f32[64,1024]{1,0:T(8,128)S(1)}, u32[]{:S(2)}, u32[]{:S(2)}) %collective-permute-start.27) | collective-permute-done | bytes 262176 | tf_op jit(solution)/shard_map/ppermute | solution.py:16
  198.0 3.3 %fusion.4 = f32[1,64,1024]{2,0,1:T(1,128)S(1)} fusion(f32[12,64,1024]{2,1,0:T(8,128)S(1)} %bitcast_dynamic-update-slice_fusion, s32[12]{0:T(128)S(1)} %copy-done.8, s32[]{:T(128)} %bitcast.23), kind=kOutput, calls=%fused_computation.8 | convolution fusion | flops 9437196 | bytes 3407924 | tf_op jit(solution)/shard_map/ko,orp->krp/dot_general | solution.py:55
  201.6 7.8 %collective-permute-start.28 = (f32[64,1024]{1,0:T(8,128)S(1)}, f32[64,1024]{1,0:T(8,128)S(1)}, u32[]{:S(2)}, u32[]{:S(2)}) collective-permute-start(f32[64,1024]{1,0:T(8,128)S(1)} %convolution_bitcast_fusion.2), channel_id=1, source_target_pairs={{0,1},{1,0},{2,3},{3,2},{4,5},{5,4},{6,7},{7,6},{8,9},{9,8},{10,11... | collective-permute-start | bytes 786440 | tf_op jit(solution)/shard_map/ppermute | solution.py:10
  211.0 3.2 %fusion.6 = f32[4,64,1024]{2,0,1:T(4,128)S(1)} fusion(f32[12,64,1024]{2,1,0:T(8,128)S(1)} %bitcast_dynamic-update-slice_fusion.12, s32[12]{0:T(128)S(1)} %copy-done.8, s32[4]{0:T(128)S(1)} %fusion.35), kind=kOutput, calls=%fused_computation.10 | convolution fusion | flops 37748784 | bytes 4194368 | tf_op jit(solution)/shard_map/ko,orp->krp/dot_general | solution.py:55
  214.2 5.8 %collective-permute-done.29 = f32[64,1024]{1,0:T(8,128)S(1)} collective-permute-done((f32[64,1024]{1,0:T(8,128)S(1)}, f32[64,1024]{1,0:T(8,128)S(1)}, u32[]{:S(2)}, u32[]{:S(2)}) %collective-permute-start.29) | collective-permute-done | bytes 262176 | tf_op jit(solution)/shard_map/ppermute | solution.py:10
  221.0 1.4 convolution_bitcast_fusion.3
  222.4 2.9 %collective-permute-start.13 = (f32[64,1024]{1,0:T(8,128)S(1)}, f32[64,1024]{1,0:T(8,128)S(1)}, u32[]{:S(2)}, u32[]{:S(2)}) collective-permute-start(f32[64,1024]{1,0:T(8,128)S(1)} %convolution_bitcast_fusion.3), channel_id=1, source_target_pairs={{0,1},{1,0},{2,3},{3,2},{4,5},{5,4},{6,7},{7,6},{8,9},{9,8},{10,11... | collective-permute-start | bytes 786440 | tf_op jit(solution)/shard_map/ppermute | solution.py:10
  225.3 5.3 %collective-permute-done.30 = f32[64,1024]{1,0:T(8,128)S(1)} collective-permute-done((f32[64,1024]{1,0:T(8,128)S(1)}, f32[64,1024]{1,0:T(8,128)S(1)}, u32[]{:S(2)}, u32[]{:S(2)}) %collective-permute-start.30) | collective-permute-done | bytes 262176 | tf_op jit(solution)/shard_map/ppermute | solution.py:10
  231.6 5.0 %fusion.38 = f32[2,1024,512]{1,2,0:T(8,128)} fusion(f32[2,64,1024]{2,1,0:T(8,128)S(1)} %convolution_bitcast_fusion, f32[2,512,64]{1,2,0:T(8,128)S(1)} %copy-done.4), kind=kOutput, calls=%fused_computation.90 | convolution fusion | flops 805306368 | bytes 4980736 | tf_op jit(solution)/shard_map/lnr,lrp->lnp/dot_general | solution.py:119
  236.6 8.5 %pad_maximum_fusion = f32[3072,1024]{1,0:T(8,128)} fusion(f32[1024,1024]{1,0:T(8,128)} %collective-permute-done.32, f32[1024,1024]{1,0:T(8,128)S(1)} %copy-done.3, f32[1024,1024]{1,0:T(8,128)} %collective-permute-done.31), kind=kLoop, calls=%fused_computation.2 | loop fusion | flops 6291456 | bytes 25165824 | tf_op jit(solution)/shard_map/concatenate | solution.py:28
  245.2 11.4 %gather_fusion.1 = f32[6,512,1024]{2,1,0:T(8,128)} fusion(f32[6,512,1024]{2,1,0:T(8,128)} %bitcast.108, s32[1024]{0:T(1024)S(1)} %pad_clamp_fusion), kind=kCustom, calls=%fused_computation.1 | custom fusion | bytes 25165848 | tf_op jit(solution)/shard_map/jit(_take)/gather | solution.py:123
  256.5 26.7 %bitcast_add_fusion = f32[2,1024,512]{1,2,0:T(8,128)} fusion(f32[2,1024,512]{1,2,0:T(8,128)} %fusion.38, f32[2,3,512,512]{3,2,1,0:T(8,128)} %param.24, f32[2,3,512,1024]{3,2,1,0:T(8,128)} %bitcast.107, pred[2,3]{1,0:T(4,128)(4,1)S(1)} %get-tuple-element.16), kind=kOutput, calls=%fused_computation.7 | convolution fusion | flops 19331547136 | bytes 27262982 | tf_op jit(solution)/shard_map/lmab,lmbp->lap/dot_general | solution.py:126
  (94 shorter events, 12.5 us)
Async XLA Ops:
  0.0 30.0 %copy-start = (f32[64,64,64]{2,1,0:T(8,128)S(1)}, f32[64,64,64]{2,1,0:T(8,128)}, u32[]{:S(2)}) copy-start(f32[64,64,64]{2,1,0:T(8,128)} %param.17) | copy-start | bytes 3145732
  0.0 14.9 %copy-start.5 = (f32[2,64,64]{2,1,0:T(8,128)S(1)}, f32[2,64,64]{2,1,0:T(8,128)}, u32[]{:S(2)}) copy-start(f32[2,64,64]{2,1,0:T(8,128)} %param.16) | copy-start | bytes 98308
  0.0 15.5 %copy-start.10 = (s32[4]{0:T(128)S(1)}, s32[4]{0:T(128)}, u32[]{:S(2)}) copy-start(s32[4]{0:T(128)} %param.19) | copy-start | bytes 52
  0.0 15.5 %copy-start.9 = (s32[2,3]{1,0:T(2,128)S(1)}, s32[2,3]{1,0:T(2,128)}, u32[]{:S(2)}) copy-start(s32[2,3]{1,0:T(2,128)} %param.25) | copy-start | bytes 76
  0.0 15.6 %copy-start.2 = (s32[64]{0:T(128)S(1)}, s32[64]{0:T(128)}, u32[]{:S(2)}) copy-start(s32[64]{0:T(128)} %param.20) | copy-start | bytes 772
  0.0 236.6 %collective-permute-start.31 = (f32[1024,1024]{1,0:T(8,128)}, f32[1024,1024]{1,0:T(8,128)}, u32[]{:S(2)}, u32[]{:S(2)}) collective-permute-start(f32[1024,1024]{1,0:T(8,128)} %param.14), channel_id=1, source_target_pairs={{0,1},{1,2},{2,3},{3,4},{4,5},{5,6},{6,7},{7,8},{8,9},{9,10},{10,1... | collective-permute-start | bytes 12582920 | tf_op jit(solution)/shard_map/ppermute | solution.py:26
  2.1 234.5 %collective-permute-start.32 = (f32[1024,1024]{1,0:T(8,128)}, f32[1024,1024]{1,0:T(8,128)}, u32[]{:S(2)}, u32[]{:S(2)}) collective-permute-start(f32[1024,1024]{1,0:T(8,128)} %param.14), channel_id=1, source_target_pairs={{1,0},{2,1},{3,2},{4,3},{5,4},{6,5},{7,6},{8,7},{9,8},{10,9},{11,1... | collective-permute-start | bytes 12582920 | tf_op jit(solution)/shard_map/ppermute | solution.py:27
  10.0 10.5 %copy-start.11 = (s32[16]{0:T(128)S(1)}, s32[16]{0:T(128)}, u32[]{:S(2)}) copy-start(s32[16]{0:T(128)} %param.23) | copy-start | bytes 196
  15.3 1.6 collective-permute-start
  17.0 15.3 %collective-permute-start.1 = (f32[64,1024]{1,0:T(8,128)S(1)}, f32[64,1024]{1,0:T(8,128)S(1)}, u32[]{:S(2)}, u32[]{:S(2)}) collective-permute-start(f32[64,1024]{1,0:T(8,128)S(1)} %add.135), channel_id=1, source_target_pairs={{0,14},{1,15},{2,16},{3,17},{4,18},{5,19},{6,20},{7,21},{8,22},{9,... | collective-permute-start | bytes 786440 | tf_op jit(solution)/shard_map/ppermute | solution.py:16
  21.6 71.8 %collective-permute-start.7 = (f32[64,1024]{1,0:T(8,128)S(1)}, f32[64,1024]{1,0:T(8,128)S(1)}, u32[]{:S(2)}, u32[]{:S(2)}) collective-permute-start(f32[64,1024]{1,0:T(8,128)S(1)} %add.135), channel_id=1, source_target_pairs={{4,0},{5,1},{6,2},{7,3},{8,4},{9,5},{10,6},{11,7},{12,8},{13,9},{1... | collective-permute-start | bytes 786440 | tf_op jit(solution)/shard_map/ppermute | solution.py:16
  27.0 18.5 %collective-permute-start.2 = (f32[64,1024]{1,0:T(8,128)S(1)}, f32[64,1024]{1,0:T(8,128)S(1)}, u32[]{:S(2)}, u32[]{:S(2)}) collective-permute-start(f32[64,1024]{1,0:T(8,128)S(1)} %add.135), channel_id=1, source_target_pairs={{0,12},{1,13},{2,14},{3,15},{4,16},{5,17},{6,18},{7,19},{8,20},{9,... | collective-permute-start | bytes 786440 | tf_op jit(solution)/shard_map/ppermute | solution.py:16
  32.3 24.6 %collective-permute-start.3 = (f32[64,1024]{1,0:T(8,128)S(1)}, f32[64,1024]{1,0:T(8,128)S(1)}, u32[]{:S(2)}, u32[]{:S(2)}) collective-permute-start(f32[64,1024]{1,0:T(8,128)S(1)} %add.135), channel_id=1, source_target_pairs={{0,10},{1,11},{2,12},{3,13},{4,14},{5,15},{6,16},{7,17},{8,18},{9,... | collective-permute-start | bytes 786440 | tf_op jit(solution)/shard_map/ppermute | solution.py:16
  45.5 13.4 %collective-permute-start.4 = (f32[64,1024]{1,0:T(8,128)S(1)}, f32[64,1024]{1,0:T(8,128)S(1)}, u32[]{:S(2)}, u32[]{:S(2)}) collective-permute-start(f32[64,1024]{1,0:T(8,128)S(1)} %add.135), channel_id=1, source_target_pairs={{0,8},{1,9},{2,10},{3,11},{4,12},{5,13},{6,14},{7,15},{8,16},{9,17... | collective-permute-start | bytes 786440 | tf_op jit(solution)/shard_map/ppermute | solution.py:16
  56.9 20.6 %collective-permute-start.5 = (f32[64,1024]{1,0:T(8,128)S(1)}, f32[64,1024]{1,0:T(8,128)S(1)}, u32[]{:S(2)}, u32[]{:S(2)}) collective-permute-start(f32[64,1024]{1,0:T(8,128)S(1)} %add.135), channel_id=1, source_target_pairs={{0,6},{1,7},{2,8},{3,9},{4,10},{5,11},{6,12},{7,13},{8,14},{9,15},... | collective-permute-start | bytes 786440 | tf_op jit(solution)/shard_map/ppermute | solution.py:16
  58.9 18.7 %collective-permute-start.6 = (f32[64,1024]{1,0:T(8,128)S(1)}, f32[64,1024]{1,0:T(8,128)S(1)}, u32[]{:S(2)}, u32[]{:S(2)}) collective-permute-start(f32[64,1024]{1,0:T(8,128)S(1)} %add.135), channel_id=1, source_target_pairs={{0,4},{1,5},{2,6},{3,7},{4,8},{5,9},{6,10},{7,11},{8,12},{9,13},{1... | collective-permute-start | bytes 786440 | tf_op jit(solution)/shard_map/ppermute | solution.py:16
  77.6 8.1 %collective-permute-start.14 = (f32[64,1024]{1,0:T(8,128)S(1)}, f32[64,1024]{1,0:T(8,128)S(1)}, u32[]{:S(2)}, u32[]{:S(2)}) collective-permute-start(f32[64,1024]{1,0:T(8,128)S(1)} %fusion.20), channel_id=1, source_target_pairs={{0,2},{1,3},{2,0},{3,1},{4,6},{5,7},{6,4},{7,5},{8,10},{9,11},{10,... | collective-permute-start | bytes 786440 | tf_op jit(solution)/shard_map/ppermute | solution.py:10
  77.6 17.8 %collective-permute-start.8 = (f32[64,1024]{1,0:T(8,128)S(1)}, f32[64,1024]{1,0:T(8,128)S(1)}, u32[]{:S(2)}, u32[]{:S(2)}) collective-permute-start(f32[64,1024]{1,0:T(8,128)S(1)} %add.135), channel_id=1, source_target_pairs={{6,0},{7,1},{8,2},{9,3},{10,4},{11,5},{12,6},{13,7},{14,8},{15,9},... | collective-permute-start | bytes 786440 | tf_op jit(solution)/shard_map/ppermute | solution.py:16
  85.7 28.2 %collective-permute-start.9 = (f32[64,1024]{1,0:T(8,128)S(1)}, f32[64,1024]{1,0:T(8,128)S(1)}, u32[]{:S(2)}, u32[]{:S(2)}) collective-permute-start(f32[64,1024]{1,0:T(8,128)S(1)} %add.135), channel_id=1, source_target_pairs={{8,0},{9,1},{10,2},{11,3},{12,4},{13,5},{14,6},{15,7},{16,8},{17,9... | collective-permute-start | bytes 786440 | tf_op jit(solution)/shard_map/ppermute | solution.py:16
  93.4 9.8 %collective-permute-start.15 = (f32[64,1024]{1,0:T(8,128)S(1)}, f32[64,1024]{1,0:T(8,128)S(1)}, u32[]{:S(2)}, u32[]{:S(2)}) collective-permute-start(f32[64,1024]{1,0:T(8,128)S(1)} %add.144), channel_id=1, source_target_pairs={{0,4},{1,5},{2,6},{3,7},{4,0},{5,1},{6,2},{7,3},{8,12},{9,13},{10,... | collective-permute-start | bytes 786440 | tf_op jit(solution)/shard_map/ppermute | solution.py:10
  95.3 19.9 %collective-permute-start.10 = (f32[64,1024]{1,0:T(8,128)S(1)}, f32[64,1024]{1,0:T(8,128)S(1)}, u32[]{:S(2)}, u32[]{:S(2)}) collective-permute-start(f32[64,1024]{1,0:T(8,128)S(1)} %add.135), channel_id=1, source_target_pairs={{10,0},{11,1},{12,2},{13,3},{14,4},{15,5},{16,6},{17,7},{18,8},{19... | collective-permute-start | bytes 786440 | tf_op jit(solution)/shard_map/ppermute | solution.py:16
  103.1 106.4 %collective-permute-start.12 = (f32[64,1024]{1,0:T(8,128)S(1)}, f32[64,1024]{1,0:T(8,128)S(1)}, u32[]{:S(2)}, u32[]{:S(2)}) collective-permute-start(f32[64,1024]{1,0:T(8,128)S(1)} %add.135), channel_id=1, source_target_pairs={{14,0},{15,1},{16,2},{17,3},{18,4},{19,5},{20,6},{21,7},{22,8},{23... | collective-permute-start | bytes 786440 | tf_op jit(solution)/shard_map/ppermute | solution.py:16
  113.9 8.4 %collective-permute-start.16 = (f32[64,1024]{1,0:T(8,128)S(1)}, f32[64,1024]{1,0:T(8,128)S(1)}, u32[]{:S(2)}, u32[]{:S(2)}) collective-permute-start(f32[64,1024]{1,0:T(8,128)S(1)} %add.145), channel_id=1, source_target_pairs={{0,56},{1,57},{2,58},{3,59},{4,60},{5,61},{6,62},{7,63},{8,64},{9,... | collective-permute-start | bytes 786440 | tf_op jit(solution)/shard_map/ppermute | solution.py:16
  115.2 12.3 %collective-permute-start.17 = (f32[64,1024]{1,0:T(8,128)S(1)}, f32[64,1024]{1,0:T(8,128)S(1)}, u32[]{:S(2)}, u32[]{:S(2)}) collective-permute-start(f32[64,1024]{1,0:T(8,128)S(1)} %add.145), channel_id=1, source_target_pairs={{0,48},{1,49},{2,50},{3,51},{4,52},{5,53},{6,54},{7,55},{8,56},{9,... | collective-permute-start | bytes 786440 | tf_op jit(solution)/shard_map/ppermute | solution.py:16
  119.7 78.3 %copy-start.8 = (s32[12]{0:T(128)S(1)}, s32[12]{0:T(128)}, u32[]{:S(2)}) copy-start(s32[12]{0:T(128)} %constant.129.clone) | copy-start | bytes 148
  122.3 12.9 %collective-permute-start.18 = (f32[64,1024]{1,0:T(8,128)S(1)}, f32[64,1024]{1,0:T(8,128)S(1)}, u32[]{:S(2)}, u32[]{:S(2)}) collective-permute-start(f32[64,1024]{1,0:T(8,128)S(1)} %add.145), channel_id=1, source_target_pairs={{0,40},{1,41},{2,42},{3,43},{4,44},{5,45},{6,46},{7,47},{8,48},{9,... | collective-permute-start | bytes 786440 | tf_op jit(solution)/shard_map/ppermute | solution.py:16
  127.6 15.5 %collective-permute-start.19 = (f32[64,1024]{1,0:T(8,128)S(1)}, f32[64,1024]{1,0:T(8,128)S(1)}, u32[]{:S(2)}, u32[]{:S(2)}) collective-permute-start(f32[64,1024]{1,0:T(8,128)S(1)} %add.145), channel_id=1, source_target_pairs={{0,32},{1,33},{2,34},{3,35},{4,36},{5,37},{6,38},{7,39},{8,40},{9,... | collective-permute-start | bytes 786440 | tf_op jit(solution)/shard_map/ppermute | solution.py:16
  135.2 12.0 %collective-permute-start.20 = (f32[64,1024]{1,0:T(8,128)S(1)}, f32[64,1024]{1,0:T(8,128)S(1)}, u32[]{:S(2)}, u32[]{:S(2)}) collective-permute-start(f32[64,1024]{1,0:T(8,128)S(1)} %add.145), channel_id=1, source_target_pairs={{0,24},{1,25},{2,26},{3,27},{4,28},{5,29},{6,30},{7,31},{8,32},{9,... | collective-permute-start | bytes 786440 | tf_op jit(solution)/shard_map/ppermute | solution.py:16
  143.0 11.2 %collective-permute-start.21 = (f32[64,1024]{1,0:T(8,128)S(1)}, f32[64,1024]{1,0:T(8,128)S(1)}, u32[]{:S(2)}, u32[]{:S(2)}) collective-permute-start(f32[64,1024]{1,0:T(8,128)S(1)} %add.145), channel_id=1, source_target_pairs={{0,16},{1,17},{2,18},{3,19},{4,20},{5,21},{6,22},{7,23},{8,24},{9,... | collective-permute-start | bytes 786440 | tf_op jit(solution)/shard_map/ppermute | solution.py:16
  147.1 11.8 %collective-permute-start.22 = (f32[64,1024]{1,0:T(8,128)S(1)}, f32[64,1024]{1,0:T(8,128)S(1)}, u32[]{:S(2)}, u32[]{:S(2)}) collective-permute-start(f32[64,1024]{1,0:T(8,128)S(1)} %add.145), channel_id=1, source_target_pairs={{16,0},{17,1},{18,2},{19,3},{20,4},{21,5},{22,6},{23,7},{24,8},{25... | collective-permute-start | bytes 786440 | tf_op jit(solution)/shard_map/ppermute | solution.py:16
  154.3 13.5 %collective-permute-start.23 = (f32[64,1024]{1,0:T(8,128)S(1)}, f32[64,1024]{1,0:T(8,128)S(1)}, u32[]{:S(2)}, u32[]{:S(2)}) collective-permute-start(f32[64,1024]{1,0:T(8,128)S(1)} %add.145), channel_id=1, source_target_pairs={{24,0},{25,1},{26,2},{27,3},{28,4},{29,5},{30,6},{31,7},{32,8},{33... | collective-permute-start | bytes 786440 | tf_op jit(solution)/shard_map/ppermute | solution.py:16
  158.9 16.5 %collective-permute-start.24 = (f32[64,1024]{1,0:T(8,128)S(1)}, f32[64,1024]{1,0:T(8,128)S(1)}, u32[]{:S(2)}, u32[]{:S(2)}) collective-permute-start(f32[64,1024]{1,0:T(8,128)S(1)} %add.145), channel_id=1, source_target_pairs={{32,0},{33,1},{34,2},{35,3},{36,4},{37,5},{38,6},{39,7},{40,8},{41... | collective-permute-start | bytes 786440 | tf_op jit(solution)/shard_map/ppermute | solution.py:16
  167.8 18.4 %collective-permute-start.25 = (f32[64,1024]{1,0:T(8,128)S(1)}, f32[64,1024]{1,0:T(8,128)S(1)}, u32[]{:S(2)}, u32[]{:S(2)}) collective-permute-start(f32[64,1024]{1,0:T(8,128)S(1)} %add.145), channel_id=1, source_target_pairs={{40,0},{41,1},{42,2},{43,3},{44,4},{45,5},{46,6},{47,7},{48,8},{49... | collective-permute-start | bytes 786440 | tf_op jit(solution)/shard_map/ppermute | solution.py:16
  175.5 13.4 %collective-permute-start.26 = (f32[64,1024]{1,0:T(8,128)S(1)}, f32[64,1024]{1,0:T(8,128)S(1)}, u32[]{:S(2)}, u32[]{:S(2)}) collective-permute-start(f32[64,1024]{1,0:T(8,128)S(1)} %add.145), channel_id=1, source_target_pairs={{48,0},{49,1},{50,2},{51,3},{52,4},{53,5},{54,6},{55,7},{56,8},{57... | collective-permute-start | bytes 786440 | tf_op jit(solution)/shard_map/ppermute | solution.py:16
  176.8 24.4 %copy-start.7 = (f32[1,64,64]{2,1,0:T(8,128)S(1)}, f32[1,64,64]{2,1,0:T(8,128)}, u32[]{:S(2)}) copy-start(f32[1,64,64]{2,1,0:T(8,128)} %param.21) | copy-start | bytes 49156
  186.2 11.8 %collective-permute-start.27 = (f32[64,1024]{1,0:T(8,128)S(1)}, f32[64,1024]{1,0:T(8,128)S(1)}, u32[]{:S(2)}, u32[]{:S(2)}) collective-permute-start(f32[64,1024]{1,0:T(8,128)S(1)} %add.145), channel_id=1, source_target_pairs={{56,0},{57,1},{58,2},{59,3},{60,4},{61,5},{62,6},{63,7},{64,8},{65... | collective-permute-start | bytes 786440 | tf_op jit(solution)/shard_map/ppermute | solution.py:16
  188.9 20.6 %collective-permute-start.11 = (f32[64,1024]{1,0:T(8,128)S(1)}, f32[64,1024]{1,0:T(8,128)S(1)}, u32[]{:S(2)}, u32[]{:S(2)}) collective-permute-start(f32[64,1024]{1,0:T(8,128)S(1)} %add.135), channel_id=1, source_target_pairs={{12,0},{13,1},{14,2},{15,3},{16,4},{17,5},{18,6},{19,7},{20,8},{21... | collective-permute-start | bytes 786440 | tf_op jit(solution)/shard_map/ppermute | solution.py:16
  201.6 9.0 %collective-permute-start.28 = (f32[64,1024]{1,0:T(8,128)S(1)}, f32[64,1024]{1,0:T(8,128)S(1)}, u32[]{:S(2)}, u32[]{:S(2)}) collective-permute-start(f32[64,1024]{1,0:T(8,128)S(1)} %convolution_bitcast_fusion.2), channel_id=1, source_target_pairs={{0,1},{1,0},{2,3},{3,2},{4,5},{5,4},{6,7},{7,6},{8,9},{9,8},{10,11... | collective-permute-start | bytes 786440 | tf_op jit(solution)/shard_map/ppermute | solution.py:10
  210.7 10.3 %copy-start.6 = (f32[4,64,64]{2,1,0:T(8,128)S(1)}, f32[4,64,64]{2,1,0:T(8,128)}, u32[]{:S(2)}) copy-start(f32[4,64,64]{2,1,0:T(8,128)} %param.18) | copy-start | bytes 196612
  210.7 9.3 %collective-permute-start.29 = (f32[64,1024]{1,0:T(8,128)S(1)}, f32[64,1024]{1,0:T(8,128)S(1)}, u32[]{:S(2)}, u32[]{:S(2)}) collective-permute-start(f32[64,1024]{1,0:T(8,128)S(1)} %add.148), channel_id=1, source_target_pairs={{0,2},{1,3},{2,0},{3,1},{4,6},{5,7},{6,4},{7,5},{8,10},{9,11},{10,... | collective-permute-start | bytes 786440 | tf_op jit(solution)/shard_map/ppermute | solution.py:10
  214.2 17.4 %copy-start.4 = (f32[2,512,64]{1,2,0:T(8,128)S(1)}, f32[2,512,64]{1,2,0:T(8,128)}, u32[]{:S(2)}) copy-start(f32[2,512,64]{1,2,0:T(8,128)} %param.15) | copy-start | bytes 786436
  220.1 10.5 %collective-permute-start.30 = (f32[64,1024]{1,0:T(8,128)S(1)}, f32[64,1024]{1,0:T(8,128)S(1)}, u32[]{:S(2)}, u32[]{:S(2)}) collective-permute-start(f32[64,1024]{1,0:T(8,128)S(1)} %add.149), channel_id=1, source_target_pairs={{0,4},{1,5},{2,6},{3,7},{4,0},{5,1},{6,2},{7,3},{8,12},{9,13},{10,... | collective-permute-start | bytes 786440 | tf_op jit(solution)/shard_map/ppermute | solution.py:10
  222.4 8.6 %collective-permute-start.13 = (f32[64,1024]{1,0:T(8,128)S(1)}, f32[64,1024]{1,0:T(8,128)S(1)}, u32[]{:S(2)}, u32[]{:S(2)}) collective-permute-start(f32[64,1024]{1,0:T(8,128)S(1)} %convolution_bitcast_fusion.3), channel_id=1, source_target_pairs={{0,1},{1,0},{2,3},{3,2},{4,5},{5,4},{6,7},{7,6},{8,9},{9,8},{10,11... | collective-permute-start | bytes 786440 | tf_op jit(solution)/shard_map/ppermute | solution.py:10
  231.0 5.6 %copy-start.3 = (f32[1024,1024]{1,0:T(8,128)S(1)}, f32[1024,1024]{1,0:T(8,128)}, u32[]{:S(2)}) copy-start(f32[1024,1024]{1,0:T(8,128)} %param.14) | copy-start | bytes 12582916
  256.5 26.7 %copy-start.1 = (f32[64,64,64]{2,1,0:T(8,128)S(1)}, f32[64,64,64]{2,1,0:T(8,128)}, u32[]{:S(2)}) copy-start(f32[64,64,64]{2,1,0:T(8,128)} %param.17) | copy-start | bytes 3145732
where the time goes:
time: 289 us; the launch traced here: 283 us
  starting transfers between devices  121 us (42%)
  waiting for transfers between devices  91.2 us (32%)
  matrix products  46.7 us (16%)
  local copies, waits for them, and re-layouts  13.2 us (5%)
  other arithmetic  8.74 us (3%)
    ppermute x24, starting transfers between devices, shifted(): return lax.ppermute(shard, axis, pairs)  97.4 us
    ppermute x24, waiting for transfers between devices, shifted(): return lax.ppermute(shard, axis, pairs)  78.3 us
    dot_general x1, matrix products, body(): jnp.einsum('lmab,lmbp->lap', near_blocks, near_rows, precision=highest)  26.7 us
    ppermute x7, starting transfers between devices, swapped(): lax.ppermute(shard, axis, [(i, i ^ 1 << apart) for i in range(lax.axis_si...  14 us
    ppermute x7, waiting for transfers between devices, swapped(): lax.ppermute(shard, axis, [(i, i ^ 1 << apart) for i in range(lax.axis_si...  12.9 us
    gather x1, local copies, waits for them, and re-layouts, body(): jnp.take(padded, local_index.reshape(-1), axis=0)  11.4 us
    concatenate x1, other arithmetic, padded_2(): shard = jnp.concatenate([before, shard, after], axis=dim)  8.52 us
    ppermute x1, starting transfers between devices, padded_2(): after = lax.ppermute(leading, axis, down)  7.86 us
  transfers between devices with their start and end apart: 33, of which 17 were waited for; matrix products, arithmetic and copies ran while one was open for 8% of the time, Pallas kernels for 0%

commit v1 on v0

v1 whole, which is shorter than its diff:
```python
import functools

import jax
import jax.numpy as jnp
from jax import lax
from jax.experimental import pallas as pl
from jax.experimental.pallas import tpu as pltpu
from jax.sharding import PartitionSpec as P

HIGH = lax.Precision.HIGH
LANES = 128
SIDE = 4
CHUNKS = ((0, 1), (1, 1), (2, 2), (4, 2), (6, 2))


def permuted(shard, target):
    pairs = []
    for i in range(lax.axis_size("leaf")):
        x, y, z, core = i // 32, i // 8 % 4, i // 2 % 4, i % 2
        to = target(x, y, z, core)
        if to is not None:
            pairs.append((i, ((to[0] * 4 + to[1]) * 4 + to[2]) * 2 + to[3]))
    return lax.ppermute(shard, "leaf", pairs)


def chip_swap(shard):
    return permuted(shard, lambda x, y, z, core: (x, y, z, 1 - core))


def along_z(shard, by):
    return permuted(shard, lambda x, y, z, core: (x, y, (z + by) % 4, core))


def along_y(shard, by):
    return permuted(shard, lambda x, y, z, core: (x, (y + by) % 4, z, core))


def along_x(shard, by):
    return permuted(
        shard, lambda x, y, z, core: (x + by, y, z, core) if 0 <= x + by < 4 else None
    )


def next_line(shard, by):
    peers = lax.axis_size("leaf")
    pairs = [(i, i + 8 * by) for i in range(peers) if 0 <= i + 8 * by < peers]
    return lax.ppermute(shard, "leaf", pairs)


def across_chips(shard):
    peers = lax.axis_size("leaf")
    pairs = [(i, i + 1 if i % 2 else i - 1) for i in range(1, peers - 1)]
    return lax.ppermute(shard, "leaf", pairs)


def split(value):
    high = value.astype(jnp.bfloat16)
    low = (value - high.astype(jnp.float32)).astype(jnp.bfloat16)
    return high, low


def dot(a, b):
    return jnp.dot(a, b, preferred_element_type=jnp.float32)


def dot3(a, b):
    a_high, a_low = split(a)
    b_high, b_low = split(b)
    return dot(a_high, b_high) + (dot(a_high, b_low) + dot(a_low, b_high))


def far_kernel(index, one, two, own, other, transfer, down):
    tables = (own, other)

    def term(table, row, slot, base):
        keep = index[base + 1, slot].astype(jnp.float32)
        return table[index[base, slot]] * keep

    far_two = jnp.zeros((64, LANES), jnp.float32)
    for side in range(2):
        for half in range(2):
            left = jnp.concatenate(
                [tables[side][2 * half + i, 2][:, :64] for i in range(2)], axis=1
            )
            right = jnp.concatenate(
                [term(two, None, side * 4 + 2 * half + i, 2) for i in range(2)], axis=0
            )
            far_two += dot3(left, right)
    for j in range(SIDE):
        total = dot3(transfer[j], far_two)
        for side in range(2):
            left = jnp.concatenate([tables[side][j, 0], tables[side][j, 1]], axis=1)
            right = jnp.concatenate(
                [term(one, None, side * 16 + j * 4 + s, 0) for s in range(4)], axis=0
            )
            total += dot3(left, right)
        down[j] = total


def far_field(index, one, two, own, other, transfer):
    vmem = pl.BlockSpec(memory_space=pltpu.VMEM)
    return pl.pallas_call(
        far_kernel,
        out_shape=jax.ShapeDtypeStruct((SIDE, 64, LANES), jnp.float32),
        in_specs=[pl.BlockSpec(memory_space=pltpu.SMEM)] + [vmem] * 5,
        out_specs=vmem,
        cost_estimate=pl.CostEstimate(
            flops=120_000_000, bytes_accessed=2_000_000, transcendentals=0
        ),
        name="far_field",
    )(index, one, two, own, other, transfer)


def near_kernel(width, where, blocks, mine, chip, cross, wide, *rest):
    downs, out, high, low = rest[:width], rest[-3], rest[-2], rest[-1]
    leaf, m = pl.program_id(0), pl.program_id(1)

    @pl.when((leaf == 0) & (m == 0))
    def _():
        for source, ref in enumerate((mine, chip, cross)):
            for i in range(2):
                a, b = split(ref[pl.ds(i * 512, 512), :])
                high[2 * source + i] = a
                low[2 * source + i] = b

    slot = where[leaf * 3 + m]
    a_high, a_low = split(blocks[0, 0])
    b_high = high[slot]
    b_low = low[slot]
    total = dot(a_high, b_high) + (dot(a_high, b_low) + dot(a_low, b_high))

    @pl.when(m == 0)
    def _():
        far = [dot3(wide[...], ref[0]) for ref in downs]
        out[...] = total + (jnp.concatenate(far, axis=1) if width > 1 else far[0])

    @pl.when(m > 0)
    def _():
        out[...] += total


def near_field(first, width, where, blocks, mine, chip, cross, wide, downs, out):
    cols = width * LANES
    at = first // width
    whole = pl.BlockSpec((1024, cols), lambda l, m, w: (0, at))
    in_specs = [
        pl.BlockSpec((1, 1, 512, 512), lambda l, m, w: (l, m, 0, 0)),
        whole,
        whole,
        pl.BlockSpec((1024, cols), lambda l, m, w: (0, 0)),
        pl.BlockSpec((512, 64), lambda l, m, w: (l, 0)),
    ]
    for unit in range(first, first + width):
        in_specs.append(
            pl.BlockSpec((1, 64, LANES), lambda l, m, w, unit=unit: (w[6 + unit], 0, 0))
        )
    args = [where, blocks, mine, chip, cross, wide] + [downs] * width
    aliases = {}
    if out is not None:
        in_specs.append(pl.BlockSpec(memory_space=pl.ANY))
        aliases = {len(args): 0}
        args.append(out)
    return pl.pallas_call(
        functools.partial(near_kernel, width),
        out_shape=jax.ShapeDtypeStruct((1024, 1024), jnp.float32),
        grid_spec=pltpu.PrefetchScalarGridSpec(
            num_scalar_prefetch=1,
            grid=(2, 3),
            in_specs=in_specs,
            out_specs=pl.BlockSpec((512, cols), lambda l, m, w: (l, at)),
            scratch_shapes=[
                pltpu.VMEM((6, 512, cols), jnp.bfloat16),
                pltpu.VMEM((6, 512, cols), jnp.bfloat16),
            ],
        ),
        input_output_aliases=aliases,
        compiler_params=pltpu.CompilerParams(
            dimension_semantics=("arbitrary", "arbitrary")
        ),
        cost_estimate=pl.CostEstimate(
            flops=3_600_000_000 * width // 3,
            bytes_accessed=8_000_000,
            transcendentals=0,
        ),
        name="near_field",
    )(*args)


def body(
    probes,
    leaf_basis,
    leaf_transfer,
    cluster_transfer,
    couple_one,
    pairs_one,
    count_one,
    couple_two,
    pairs_two,
    count_two,
    near_blocks,
    near_list,
):
    device = lax.axis_index("leaf")
    core, z = device % 2, device // 2 % 4
    line = device // 8
    y, x = line % 4, line // 4
    around = jnp.arange(4, dtype=jnp.int32)

    crosses = [
        across_chips(probes[:, first * LANES : (first + width) * LANES])
        for first, width in CHUNKS
    ]

    partners = jnp.concatenate([pairs_one, pairs_two]).astype(jnp.float32)
    partners = jnp.pad(partners[None, :], ((0, 63), (0, 59)))
    couplings = jnp.stack(
        [
            jnp.concatenate([couple_one[0], couple_one[1]], axis=1),
            jnp.concatenate([couple_one[2], couple_one[3]], axis=1),
            jnp.concatenate([couple_two[0], partners], axis=1),
        ]
    )
    own_table = jnp.stack(
        [
            couplings,
            along_z(couplings, -1),
            along_z(couplings, 2),
            along_z(couplings, 1),
        ]
    )
    other_table = chip_swap(own_table)

    wide = jnp.einsum("lnr,lrs->lns", leaf_basis, leaf_transfer, precision=HIGH)
    wide = wide.reshape(1024, 64)
    part = lax.dot_general(wide, probes, (((0,), (0,)), ((), ())), precision=HIGH)
    theirs = lax.dynamic_slice_in_dim(part, (1 - core) * 512, 512, axis=1)
    mine = lax.dynamic_slice_in_dim(part, core * 512, 512, axis=1)
    mine = mine + chip_swap(theirs)

    def columns(offset):
        return lax.dynamic_slice_in_dim(mine, (z + offset) % 4 * LANES, LANES, axis=1)

    level_one = jnp.stack(
        [
            columns(0),
            along_z(columns(3), -1),
            along_z(columns(2), 2),
            along_z(columns(1), 1),
        ]
    )
    transfer = jnp.take(cluster_transfer, line * 4 + (z + around) % 4, axis=0)
    coef_two = jnp.einsum("jrs,jrp->sp", transfer, level_one, precision=HIGH)
    chip = chip_swap(probes)

    plane = jnp.stack(
        [
            coef_two,
            along_y(coef_two, -1),
            along_y(coef_two, 2),
            along_y(coef_two, 1),
        ]
    )
    all_one = jnp.concatenate([next_line(level_one, 1), level_one, next_line(level_one, -1)])
    all_two = jnp.concatenate([along_x(plane, 1), plane, along_x(plane, -1)])

    ids = jnp.stack([own_table[:, 2, 0, 64:69], other_table[:, 2, 0, 64:69]])
    ids = ids.astype(jnp.int32)
    cores = jnp.stack([core, 1 - core])
    cluster = line * 4 + (z + around) % 4
    slot_one = cores[:, None, None] * 4 + around[None, None, :]
    keep_one = slot_one < jnp.take(count_one, cluster)[None, :, None]
    id_one = ids[:, :, :4]
    at_one = (id_one // 4 - line + 1) * 4 + (id_one % 4 - z) % 4
    slot_two = (z + around)[None, :] % 4 * 2 + cores[:, None]
    keep_two = slot_two < count_two[line]
    id_two = ids[:, :, 4]
    at_two = (id_two // 4 - x + 1) * 4 + (id_two % 4 - y) % 4
    pad = ((0, 0), (0, 24))
    index = jnp.concatenate(
        [
            jnp.clip(at_one, 0, 11).reshape(1, 32),
            keep_one.astype(jnp.int32).reshape(1, 32),
            jnp.pad(jnp.clip(at_two, 0, 11).reshape(1, 8), pad),
            jnp.pad(keep_two.astype(jnp.int32).reshape(1, 8), pad),
        ]
    )

    down = far_field(index, all_one, all_two, own_table, other_table, transfer)
    back = jnp.stack(
        [down[0], along_z(down[3], -1), along_z(down[2], 2), along_z(down[1], 1)]
    )
    downs = jnp.concatenate([back, chip_swap(back)])

    local = near_list.reshape(-1) - 2 * device
    before = jnp.where(core == 0, 4, 2) + local + 2
    after = jnp.where(core == 0, 2, 4) + local - 2
    source = jnp.where(local < 0, before, jnp.where(local > 1, after, local))
    units = jnp.arange(8, dtype=jnp.int32)
    unit_at = jnp.where(units // 4 == core, 0, 4) + (units % 4 - z) % 4
    where = jnp.concatenate([source, unit_at]).astype(jnp.int32)
    out = None
    for (first, width), cross in zip(CHUNKS, crosses):
        out = near_field(
            first, width, where, near_blocks, probes, chip, cross, wide, downs, out
        )
    return out


def solution(mesh):
    return jax.shard_map(
        body,
        mesh=mesh,
        in_specs=(
            P("leaf", None),
            P("leaf", None, None),
            P("leaf", None, None),
            P(),
            P("leaf", None, None),
            P("leaf"),
            P(),
            P("leaf", None, None),
            P("leaf"),
            P(),
            P("leaf", None, None, None),
            P("leaf", None),
        ),
        out_specs=P("leaf", None),
        check_vma=False,
    )
```

time: 289 us -> 151 us (0.52); the launches traced: 283 us -> 150 us
  waiting for transfers between devices: 91.2 us -> 19.7 us
  starting transfers between devices: 121 us -> 52.6 us
  Pallas kernels: 0 us -> 52 us
  matrix products: 46.7 us -> 5.62 us
  other arithmetic: 8.74 us -> 5.52 us
    ppermute x33 -> x25, waiting for transfers between devices: 91.2 us -> 19.7 us  [the longest x18 8.89 us: permuted(): return lax.ppermute(shard, 'leaf', pairs)]
    ppermute x33 -> x25, starting transfers between devices: 121 us -> 52.6 us  [the longest x5 23.1 us: across_chips(): return lax.ppermute(shard, 'leaf', pairs)]
    pallas_call x0 -> x6, Pallas kernels: none -> 52 us  [the longest x5 49.1 us: near_field(): pl.pallas_call(functools.partial(near_kernel, width), out_shape=jax.Shape...]
    dot_general x11 -> x3, matrix products: 46.7 us -> 5.62 us  [the longest x1 3.81 us: body(): lax.dot_general(wide, probes, (((0,), (0,)), ((), ())), precision=HIGH)]
    gather x3 -> x2, local copies, waits for them, and re-layouts: 12.6 us -> 1.2 us  [the longest x1 0.64 us: body(): keep_one = slot_one < jnp.take(count_one, cluster)[None, :, None]]
    concatenate x1 -> x2, other arithmetic: 8.52 us -> 1.18 us  [the longest x1 0.6 us: body(): jnp.concatenate([jnp.clip(at_one, 0, 11).reshape(1, 32), keep_one.astype(...]
    slice x0 -> x6, local copies, waits for them, and re-layouts: none -> 7.04 us  [the longest x2 5.86 us: body(): probes[:, first * LANES:(first + width) * LANES]]
  transfers between devices with their start and end apart: 33 -> 25, of which waited for: 17 -> 6; matrix products, arithmetic and copies ran while one was open for 8% -> 12% of each run, Pallas kernels for 0% -> 28%
where the time goes in v1:
time: 151 us; the launch traced here: 150 us
  starting transfers between devices  52.6 us (35%)
  Pallas kernels  52 us (34%)
  waiting for transfers between devices  19.7 us (13%)
  local copies, waits for them, and re-layouts  12.9 us (9%)
  matrix products  5.62 us (4%)
  other arithmetic  5.52 us (4%)
    pallas_call x5, Pallas kernels, near_field(): pl.pallas_call(functools.partial(near_kernel, width), out_shape=jax.Shape...  49.1 us
    ppermute x5, starting transfers between devices, across_chips(): return lax.ppermute(shard, 'leaf', pairs)  23.1 us
    ppermute x18, starting transfers between devices, permuted(): return lax.ppermute(shard, 'leaf', pairs)  22.5 us
    ppermute x18, waiting for transfers between devices, permuted(): return lax.ppermute(shard, 'leaf', pairs)  8.89 us
    ppermute x5, waiting for transfers between devices, across_chips(): return lax.ppermute(shard, 'leaf', pairs)  7.77 us
    ppermute x2, starting transfers between devices, next_line(): return lax.ppermute(shard, 'leaf', pairs)  7.05 us
    slice x2, local copies, waits for them, and re-layouts, body(): probes[:, first * LANES:(first + width) * LANES]  5.86 us
    dot_general x1, matrix products, body(): lax.dot_general(wide, probes, (((0,), (0,)), ((), ())), precision=HIGH)  3.81 us
  transfers between devices with their start and end apart: 25, of which 6 were waited for; matrix products, arithmetic and copies ran while one was open for 12% of the time, Pallas kernels for 28%

profile of v1, /device:TPU:2, one launch (start us, length us, event | category | flops | bytes accessed | tf_op | source)
XLA Modules:
  0.0 149.6 jit_solution(3834120088604677041)
XLA Ops:
  0.0 1.0 slice_bitcast_fusion.6
  1.6 0.7 add_convert_fusion
  2.4 0.8 fusion
  3.3 0.6 fusion.22
  3.9 4.0 %collective-permute-start.2 = (f32[3,64,128]{2,1,0:T(8,128)}, f32[3,64,128]{2,1,0:T(8,128)S(1)}, u32[]{:S(2)}, u32[]{:S(2)}) collective-permute-start(f32[3,64,128]{2,1,0:T(8,128)} %get-tuple-element.28), channel_id=1, source_target_pairs={{0,6},{1,7},{2,0},{3,1},{4,2},{5,3},{6,4},{7,5},{8,14},{9,15},{10,... | collective-permute-start | bytes 294920 | tf_op jit(solution)/shard_map/ppermute | solution.py:23
  8.0 1.5 %fusion.27 = f32[2,512,64]{2,1,0:T(8,128)S(1)} fusion(f32[2,512,64]{1,2,0:T(8,128)} %param.13, f32[2,64,64]{2,1,0:T(8,128)} %param.14), kind=kOutput, calls=%fused_computation.121 | convolution fusion | flops 25165824 | bytes 557056 | tf_op jit(solution)/shard_map/lnr,lrs->lns/dot_general | solution.py:233
  9.5 3.8 %fusion.28 = f32[64,1024]{1,0:T(8,128)S(1)} fusion(f32[1024,64]{1,0:T(8,128)S(1)} %bitcast.65, f32[1024,1024]{1,0:T(8,128)} %mine.9), kind=kOutput, calls=%fused_computation.122 | convolution fusion | flops 402653184 | bytes 4718592 | tf_op jit(solution)/shard_map/dot_general | solution.py:235
  13.5 2.3 %fusion.24 = (f32[1024,128]{1,0:T(8,128)}, f32[1024,128]{1,0:T(8,128)}) fusion(f32[1024,1024]{1,0:T(8,128)} %mine.9), kind=kLoop, calls=%fused_computation.118 | loop fusion | bytes 2097152 | tf_op jit(solution)/shard_map/slice | solution.py:210
  15.8 3.6 %fusion.25 = (f32[1024,256]{1,0:T(8,128)}, f32[1024,256]{1,0:T(8,128)}, f32[1024,256]{1,0:T(8,128)}) fusion(f32[1024,1024]{1,0:T(8,128)} %mine.9), kind=kLoop, calls=%fused_computation.119 | loop fusion | bytes 6291456 | tf_op jit(solution)/shard_map/slice | solution.py:210
  20.0 0.6 gather_fusion
  21.0 0.6 dynamic_slice.21
  21.7 0.6 add_compare_fusion
  22.6 0.7 collective-permute-start.7
  23.3 3.0 %collective-permute-start.8 = (f32[64,128]{1,0:T(8,128)S(1)}, f32[64,128]{1,0:T(8,128)S(1)}, u32[]{:S(2)}, u32[]{:S(2)}) collective-permute-start(f32[64,128]{1,0:T(8,128)S(1)} %get-tuple-element.21), channel_id=1, source_target_pairs={{0,4},{1,5},{2,6},{3,7},{4,0},{5,1},{6,2},{7,3},{8,12},{9,13},{10,... | collective-permute-start | bytes 98312 | tf_op jit(solution)/shard_map/ppermute | solution.py:23
  26.2 1.3 collective-permute-start.9
  28.1 0.6 collective-permute-done.8
  28.7 2.7 %collective-permute-done.9 = f32[64,128]{1,0:T(8,128)S(1)} collective-permute-done((f32[64,128]{1,0:T(8,128)S(1)}, f32[64,128]{1,0:T(8,128)S(1)}, u32[]{:S(2)}, u32[]{:S(2)}) %collective-permute-start.9) | collective-permute-done | bytes 32800 | tf_op jit(solution)/shard_map/ppermute | solution.py:23
  31.6 3.1 %collective-permute-start.12 = (f32[64,128]{1,0:T(8,128)S(1)}, f32[64,128]{1,0:T(8,128)S(1)}, u32[]{:S(2)}, u32[]{:S(2)}) collective-permute-start(f32[64,128]{1,0:T(8,128)S(1)} %bitcast.77), channel_id=1, source_target_pairs={{0,24},{1,25},{2,26},{3,27},{4,28},{5,29},{6,30},{7,31},{8,0},{9,1... | collective-permute-start | bytes 98312 | tf_op jit(solution)/shard_map/ppermute | solution.py:23
  34.8 0.7 collective-permute-start.13
  35.5 1.0 collective-permute-start.14
  36.4 3.8 %collective-permute-start.10 = (f32[4,64,128]{2,1,0:T(8,128)S(1)}, f32[4,64,128]{2,1,0:T(8,128)S(1)}, u32[]{:S(2)}, u32[]{:S(2)}) collective-permute-start(f32[4,64,128]{2,1,0:T(8,128)S(1)} %pad_maximum_fusion.1), channel_id=1, source_target_pairs={{0,8},{1,9},{2,10},{3,11},{4,12},{5,13},{6,14},{7,15},{8,16},{9,17... | collective-permute-start | bytes 393224 | tf_op jit(solution)/shard_map/ppermute | solution.py:47
  40.2 0.9 pad_maximum_fusion.own
  41.2 3.3 %collective-permute-start.24 = (f32[1024,128]{1,0:T(8,128)}, f32[1024,128]{1,0:T(8,128)}, u32[]{:S(2)}, u32[]{:S(2)}) collective-permute-start(f32[1024,128]{1,0:T(8,128)} %get-tuple-element.9), channel_id=1, source_target_pairs={{1,2},{2,1},{3,4},{4,3},{5,6},{6,5},{7,8},{8,7},{9,10},{10,9},{11,... | collective-permute-start | bytes 1572872 | tf_op jit(solution)/shard_map/ppermute | solution.py:53
  44.7 3.3 %collective-permute-start.11 = (f32[4,64,128]{2,1,0:T(8,128)S(1)}, f32[4,64,128]{2,1,0:T(8,128)S(1)}, u32[]{:S(2)}, u32[]{:S(2)}) collective-permute-start(f32[4,64,128]{2,1,0:T(8,128)S(1)} %pad_maximum_fusion.1), channel_id=1, source_target_pairs={{8,0},{9,1},{10,2},{11,3},{12,4},{13,5},{14,6},{15,7},{16,8},{17,9... | collective-permute-start | bytes 393224 | tf_op jit(solution)/shard_map/ppermute | solution.py:47
  48.0 3.4 %collective-permute-start.15 = (f32[4,64,128]{2,1,0:T(8,128)S(1)}, f32[4,64,128]{2,1,0:T(8,128)S(1)}, u32[]{:S(2)}, u32[]{:S(2)}) collective-permute-start(f32[4,64,128]{2,1,0:T(8,128)S(1)} %pad_maximum_fusion.2), channel_id=1, source_target_pairs={{0,32},{1,33},{2,34},{3,35},{4,36},{5,37},{6,38},{7,39},{8,40},{9,... | collective-permute-start | bytes 393224 | tf_op jit(solution)/shard_map/ppermute | solution.py:23
  51.5 3.0 %collective-permute-done.11 = f32[4,64,128]{2,1,0:T(8,128)S(1)} collective-permute-done((f32[4,64,128]{2,1,0:T(8,128)S(1)}, f32[4,64,128]{2,1,0:T(8,128)S(1)}, u32[]{:S(2)}, u32[]{:S(2)}) %collective-permute-start.11) | collective-permute-done | bytes 131104 | tf_op jit(solution)/shard_map/ppermute | solution.py:47
  54.5 2.4 %collective-permute-start.16 = (f32[4,64,128]{2,1,0:T(8,128)S(1)}, f32[4,64,128]{2,1,0:T(8,128)S(1)}, u32[]{:S(2)}, u32[]{:S(2)}) collective-permute-start(f32[4,64,128]{2,1,0:T(8,128)S(1)} %pad_maximum_fusion.2), channel_id=1, source_target_pairs={{32,0},{33,1},{34,2},{35,3},{36,4},{37,5},{38,6},{39,7},{40,8},{41... | collective-permute-start | bytes 393224 | tf_op jit(solution)/shard_map/ppermute | solution.py:23
  57.1 4.3 %collective-permute-done.16 = f32[4,64,128]{2,1,0:T(8,128)S(1)} collective-permute-done((f32[4,64,128]{2,1,0:T(8,128)S(1)}, f32[4,64,128]{2,1,0:T(8,128)S(1)}, u32[]{:S(2)}, u32[]{:S(2)}) %collective-permute-start.16) | collective-permute-done | bytes 131104 | tf_op jit(solution)/shard_map/ppermute | solution.py:23
  61.4 0.8 copy-done.9
  62.8 0.6 fusion.10.index
  63.4 2.9 %far_field.1 = f32[4,64,128]{2,1,0:T(8,128)} custom-call(s32[4,32]{1,0:T(4,128)} %fusion.10.index, f32[12,64,128]{2,1,0:T(8,128)} %copy-done.7, f32[12,64,128]{2,1,0:T(8,128)} %copy-done.8, f32[4,3,64,128]{3,2,1,0:T(8,128)} %copy-done.4, f32[4,3,64,128]{3,2,1,0:T(8,128)} %copy-done.9, f32[4,64,64]{2,1,0:T(8,128)} %copy-done.5), custom_call_target="tpu_custom_call" | custom-call | flops 120000000 | bytes 2000000 | tf_op jit(solution)/shard_map/far_field/pallas_call | solution.py:102
  66.3 0.8 fusion.26
  67.1 1.2 collective-permute-start.17
  68.3 0.9 collective-permute-start.19
  69.2 0.6 pad_add_fusion.1.where
  69.8 1.3 collective-permute-done.17
  71.1 4.1 %collective-permute-start.22 = (f32[1024,256]{1,0:T(8,128)}, f32[1024,256]{1,0:T(8,128)S(1)}, u32[]{:S(2)}, u32[]{:S(2)}) collective-permute-start(f32[1024,256]{1,0:T(8,128)} %get-tuple-element.11), channel_id=1, source_target_pairs={{1,2},{2,1},{3,4},{4,3},{5,6},{6,5},{7,8},{8,7},{9,10},{10,9},{11,... | collective-permute-start | bytes 3145736 | tf_op jit(solution)/shard_map/ppermute | solution.py:53
  75.2 5.7 %collective-permute-start.21 = (f32[1024,256]{1,0:T(8,128)}, f32[1024,256]{1,0:T(8,128)}, u32[]{:S(2)}, u32[]{:S(2)}) collective-permute-start(f32[1024,256]{1,0:T(8,128)} %get-tuple-element.12), channel_id=1, source_target_pairs={{1,2},{2,1},{3,4},{4,3},{5,6},{6,5},{7,8},{8,7},{9,10},{10,9},{11,... | collective-permute-start | bytes 3145736 | tf_op jit(solution)/shard_map/ppermute | solution.py:53
  81.0 4.1 %collective-permute-start.23 = (f32[1024,128]{1,0:T(8,128)}, f32[1024,128]{1,0:T(8,128)}, u32[]{:S(2)}, u32[]{:S(2)}) collective-permute-start(f32[1024,128]{1,0:T(8,128)} %get-tuple-element.10), channel_id=1, source_target_pairs={{1,2},{2,1},{3,4},{4,3},{5,6},{6,5},{7,8},{8,7},{9,10},{10,9},{11,... | collective-permute-start | bytes 1572872 | tf_op jit(solution)/shard_map/ppermute | solution.py:53
  85.2 5.9 %collective-permute-start.1 = (f32[1024,256]{1,0:T(8,128)}, f32[1024,256]{1,0:T(8,128)}, u32[]{:S(2)}, u32[]{:S(2)}) collective-permute-start(f32[1024,256]{1,0:T(8,128)} %get-tuple-element.13), channel_id=1, source_target_pairs={{1,2},{2,1},{3,4},{4,3},{5,6},{6,5},{7,8},{8,7},{9,10},{10,9},{11,... | collective-permute-start | bytes 3145736 | tf_op jit(solution)/shard_map/ppermute | solution.py:53
  91.1 0.7 copy-done.3
  91.8 9.1 %near_field.5.rest_1_ = f32[1024,1024]{1,0:T(8,128)} custom-call(s32[14]{0:T(128)} %pad_add_fusion.1.where, f32[2,3,512,512]{3,2,1,0:T(8,128)} %blocks.9, f32[1024,1024]{1,0:T(8,128)} %mine.9, f32[1024,1024]{1,0:T(8,128)} %collective-permute-done.chip, f32[1024,128]{1,0:T(8,128)} %collective-permute-done.24.cross, f32[1024,64]{1,0:T(8,128)} %bitcast.66, ...), custom_call_target="tpu_custom_call" | custom-call | flops 1200000000 | bytes 8000000 | tf_op jit(solution)/shard_map/near_field/pallas_call | solution.py:163
  100.8 7.8 %collective-permute-done.23.cross = f32[1024,128]{1,0:T(8,128)} collective-permute-done((f32[1024,128]{1,0:T(8,128)}, f32[1024,128]{1,0:T(8,128)}, u32[]{:S(2)}, u32[]{:S(2)}) %collective-permute-start.23) | collective-permute-done | bytes 524320 | tf_op jit(solution)/shard_map/ppermute | solution.py:53
  108.6 9.1 %near_field.6.rest_2_ = f32[1024,1024]{1,0:T(8,128)} custom-call(s32[14]{0:T(128)} %pad_add_fusion.1.where, f32[2,3,512,512]{3,2,1,0:T(8,128)} %blocks.9, f32[1024,1024]{1,0:T(8,128)} %mine.9, f32[1024,1024]{1,0:T(8,128)} %collective-permute-done.chip, f32[1024,128]{1,0:T(8,128)} %collective-permute-done.23.cross, ...), custom_call_target="tpu_custom_call", output_to_operand_aliasing={{}: (7, {})} | custom-call | flops 1200000000 | bytes 8000000 | tf_op jit(solution)/shard_map/near_field/pallas_call | solution.py:163
  117.7 1.0 copy-done.6
  118.7 10.3 %near_field.7.rest_2_ = f32[1024,1024]{1,0:T(8,128)} custom-call(s32[14]{0:T(128)} %pad_add_fusion.1.where, f32[2,3,512,512]{3,2,1,0:T(8,128)} %blocks.9, f32[1024,1024]{1,0:T(8,128)} %mine.9, f32[1024,1024]{1,0:T(8,128)} %collective-permute-done.chip, f32[1024,256]{1,0:T(8,128)} %copy-done.6, f32[1024,64]{1,0:T(8,128)} %bitcast.68, ...), custom_call_target="tpu_custom_call", output_to_operand_aliasing={{}: (8, {})} | custom-call | flops 2400000000 | bytes 8000000 | tf_op jit(solution)/shard_map/near_field/pallas_call | solution.py:163
  129.0 10.3 %near_field.8.rest_2_ = f32[1024,1024]{1,0:T(8,128)} custom-call(s32[14]{0:T(128)} %pad_add_fusion.1.where, f32[2,3,512,512]{3,2,1,0:T(8,128)} %blocks.9, f32[1024,1024]{1,0:T(8,128)} %mine.9, f32[1024,1024]{1,0:T(8,128)} %collective-permute-done.chip, f32[1024,256]{1,0:T(8,128)} %collective-permute-done.21.cross, ...), custom_call_target="tpu_custom_call", output_to_operand_aliasing={{}: (8, {})} | custom-call | flops 2400000000 | bytes 8000000 | tf_op jit(solution)/shard_map/near_field/pallas_call | solution.py:163
  139.3 10.3 %near_field.9 = f32[1024,1024]{1,0:T(8,128)} custom-call(s32[14]{0:T(128)} %pad_add_fusion.1.where, f32[2,3,512,512]{3,2,1,0:T(8,128)} %blocks.9, f32[1024,1024]{1,0:T(8,128)} %mine.9, f32[1024,1024]{1,0:T(8,128)} %collective-permute-done.chip, f32[1024,256]{1,0:T(8,128)} %collective-permute-done.1.cross, ...), custom_call_target="tpu_custom_call", output_to_operand_aliasing={{}: (8, {})} | custom-call | flops 2400000000 | bytes 8000000 | tf_op jit(solution)/shard_map/near_field/pallas_call | solution.py:163
  (94 shorter events, 3.1 us)
Async XLA Ops:
  0.0 19.4 %copy-start = (f32[64,64,64]{2,1,0:T(8,128)S(1)}, f32[64,64,64]{2,1,0:T(8,128)}, u32[]{:S(2)}) copy-start(f32[64,64,64]{2,1,0:T(8,128)} %param.15) | copy-start | bytes 3145732
  3.9 30.8 %collective-permute-start.2 = (f32[3,64,128]{2,1,0:T(8,128)}, f32[3,64,128]{2,1,0:T(8,128)S(1)}, u32[]{:S(2)}, u32[]{:S(2)}) collective-permute-start(f32[3,64,128]{2,1,0:T(8,128)} %get-tuple-element.28), channel_id=1, source_target_pairs={{0,6},{1,7},{2,0},{3,1},{4,2},{5,3},{6,4},{7,5},{8,14},{9,15},{10,... | collective-permute-start | bytes 294920 | tf_op jit(solution)/shard_map/ppermute | solution.py:23
  8.0 27.5 %collective-permute-start.3 = (f32[3,64,128]{2,1,0:T(8,128)}, f32[3,64,128]{2,1,0:T(8,128)}, u32[]{:S(2)}, u32[]{:S(2)}) collective-permute-start(f32[3,64,128]{2,1,0:T(8,128)} %get-tuple-element.28), channel_id=1, source_target_pairs={{0,4},{1,5},{2,6},{3,7},{4,0},{5,1},{6,2},{7,3},{8,12},{9,13},{10,... | collective-permute-start | bytes 294920 | tf_op jit(solution)/shard_map/ppermute | solution.py:23
  9.5 9.9 %copy-start.2 = (f32[2,512,64]{2,1,0:T(8,128)}, f32[2,512,64]{2,1,0:T(8,128)S(1)}, u32[]{:S(2)}) copy-start(f32[2,512,64]{2,1,0:T(8,128)S(1)} %fusion.27) | copy-start | bytes 786436
  13.4 9.1 %collective-permute-start.6 = (f32[64,512]{1,0:T(8,128)S(1)}, f32[64,512]{1,0:T(8,128)S(1)}, u32[]{:S(2)}, u32[]{:S(2)}) collective-permute-start(f32[64,512]{1,0:T(8,128)S(1)} %constant_dynamic-slice_fusion.3), channel_id=1, source_target_pairs={{0,1},{1,0},{2,3},{3,2},{4,5},{5,4},{6,7},{7,6},{8,9},{9,8},{10,11... | collective-permute-start | bytes 393224 | tf_op jit(solution)/shard_map/ppermute | solution.py:23
  13.5 6.5 %copy-start.1 = (s32[64]{0:T(128)S(1)}, s32[64]{0:T(128)}, u32[]{:S(2)}) copy-start(s32[64]{0:T(128)} %param.18) | copy-start | bytes 772
  13.5 7.3 %copy-start.10 = (s32[2,3]{1,0:T(2,128)S(1)}, s32[2,3]{1,0:T(2,128)}, u32[]{:S(2)}) copy-start(s32[2,3]{1,0:T(2,128)} %param.23) | copy-start | bytes 76
  15.8 5.2 %copy-start.11 = (s32[16]{0:T(128)S(1)}, s32[16]{0:T(128)}, u32[]{:S(2)}) copy-start(s32[16]{0:T(128)} %param.21) | copy-start | bytes 196
  21.0 42.4 %copy-start.5 = (f32[4,64,64]{2,1,0:T(8,128)}, f32[4,64,64]{2,1,0:T(8,128)S(1)}, u32[]{:S(2)}) copy-start(f32[4,64,64]{2,1,0:T(8,128)S(1)} %broadcast_select_fusion.transfer) | copy-start | bytes 196612
  22.6 5.1 %collective-permute-start.7 = (f32[64,128]{1,0:T(8,128)S(1)}, f32[64,128]{1,0:T(8,128)S(1)}, u32[]{:S(2)}, u32[]{:S(2)}) collective-permute-start(f32[64,128]{1,0:T(8,128)S(1)} %get-tuple-element.22), channel_id=1, source_target_pairs={{0,6},{1,7},{2,0},{3,1},{4,2},{5,3},{6,4},{7,5},{8,14},{9,15},{10,... | collective-permute-start | bytes 98312 | tf_op jit(solution)/shard_map/ppermute | solution.py:23
  23.3 5.4 %collective-permute-start.8 = (f32[64,128]{1,0:T(8,128)S(1)}, f32[64,128]{1,0:T(8,128)S(1)}, u32[]{:S(2)}, u32[]{:S(2)}) collective-permute-start(f32[64,128]{1,0:T(8,128)S(1)} %get-tuple-element.21), channel_id=1, source_target_pairs={{0,4},{1,5},{2,6},{3,7},{4,0},{5,1},{6,2},{7,3},{8,12},{9,13},{10,... | collective-permute-start | bytes 98312 | tf_op jit(solution)/shard_map/ppermute | solution.py:23
  26.2 5.1 %collective-permute-start.9 = (f32[64,128]{1,0:T(8,128)S(1)}, f32[64,128]{1,0:T(8,128)S(1)}, u32[]{:S(2)}, u32[]{:S(2)}) collective-permute-start(f32[64,128]{1,0:T(8,128)S(1)} %get-tuple-element.20), channel_id=1, source_target_pairs={{0,2},{1,3},{2,4},{3,5},{4,6},{5,7},{6,0},{7,1},{8,10},{9,11},{10,... | collective-permute-start | bytes 98312 | tf_op jit(solution)/shard_map/ppermute | solution.py:23
  27.7 8.8 %collective-permute-start.4 = (f32[3,64,128]{2,1,0:T(8,128)}, f32[3,64,128]{2,1,0:T(8,128)S(1)}, u32[]{:S(2)}, u32[]{:S(2)}) collective-permute-start(f32[3,64,128]{2,1,0:T(8,128)} %get-tuple-element.28), channel_id=1, source_target_pairs={{0,2},{1,3},{2,4},{3,5},{4,6},{5,7},{6,0},{7,1},{8,10},{9,11},{10,... | collective-permute-start | bytes 294920 | tf_op jit(solution)/shard_map/ppermute | solution.py:23
  28.7 62.4 %collective-permute-start = (f32[1024,1024]{1,0:T(8,128)}, f32[1024,1024]{1,0:T(8,128)}, u32[]{:S(2)}, u32[]{:S(2)}) collective-permute-start(f32[1024,1024]{1,0:T(8,128)} %mine.9), channel_id=1, source_target_pairs={{0,1},{1,0},{2,3},{3,2},{4,5},{5,4},{6,7},{7,6},{8,9},{9,8},{10,11... | collective-permute-start | bytes 12582920 | tf_op jit(solution)/shard_map/ppermute | solution.py:23
  31.6 9.6 %collective-permute-start.12 = (f32[64,128]{1,0:T(8,128)S(1)}, f32[64,128]{1,0:T(8,128)S(1)}, u32[]{:S(2)}, u32[]{:S(2)}) collective-permute-start(f32[64,128]{1,0:T(8,128)S(1)} %bitcast.77), channel_id=1, source_target_pairs={{0,24},{1,25},{2,26},{3,27},{4,28},{5,29},{6,30},{7,31},{8,0},{9,1... | collective-permute-start | bytes 98312 | tf_op jit(solution)/shard_map/ppermute | solution.py:23
  34.8 9.8 %collective-permute-start.13 = (f32[64,128]{1,0:T(8,128)S(1)}, f32[64,128]{1,0:T(8,128)S(1)}, u32[]{:S(2)}, u32[]{:S(2)}) collective-permute-start(f32[64,128]{1,0:T(8,128)S(1)} %bitcast.78), channel_id=1, source_target_pairs={{0,16},{1,17},{2,18},{3,19},{4,20},{5,21},{6,22},{7,23},{8,24},{9,... | collective-permute-start | bytes 98312 | tf_op jit(solution)/shard_map/ppermute | solution.py:23
  35.5 9.2 %collective-permute-start.14 = (f32[64,128]{1,0:T(8,128)S(1)}, f32[64,128]{1,0:T(8,128)S(1)}, u32[]{:S(2)}, u32[]{:S(2)}) collective-permute-start(f32[64,128]{1,0:T(8,128)S(1)} %bitcast.79), channel_id=1, source_target_pairs={{0,8},{1,9},{2,10},{3,11},{4,12},{5,13},{6,14},{7,15},{8,16},{9,17... | collective-permute-start | bytes 98312 | tf_op jit(solution)/shard_map/ppermute | solution.py:23
  36.4 11.6 %collective-permute-start.10 = (f32[4,64,128]{2,1,0:T(8,128)S(1)}, f32[4,64,128]{2,1,0:T(8,128)S(1)}, u32[]{:S(2)}, u32[]{:S(2)}) collective-permute-start(f32[4,64,128]{2,1,0:T(8,128)S(1)} %pad_maximum_fusion.1), channel_id=1, source_target_pairs={{0,8},{1,9},{2,10},{3,11},{4,12},{5,13},{6,14},{7,15},{8,16},{9,17... | collective-permute-start | bytes 393224 | tf_op jit(solution)/shard_map/ppermute | solution.py:47
  41.2 22.2 %copy-start.4 = (f32[4,3,64,128]{3,2,1,0:T(8,128)}, f32[4,3,64,128]{3,2,1,0:T(8,128)S(1)}, u32[]{:S(2)}) copy-start(f32[4,3,64,128]{3,2,1,0:T(8,128)S(1)} %pad_maximum_fusion.own) | copy-start | bytes 1179652
  41.2 39.8 %collective-permute-start.24 = (f32[1024,128]{1,0:T(8,128)}, f32[1024,128]{1,0:T(8,128)}, u32[]{:S(2)}, u32[]{:S(2)}) collective-permute-start(f32[1024,128]{1,0:T(8,128)} %get-tuple-element.9), channel_id=1, source_target_pairs={{1,2},{2,1},{3,4},{4,3},{5,6},{6,5},{7,8},{8,7},{9,10},{10,9},{11,... | collective-permute-start | bytes 1572872 | tf_op jit(solution)/shard_map/ppermute | solution.py:53
  44.6 16.8 %collective-permute-start.5 = (f32[4,3,64,128]{3,2,1,0:T(8,128)S(1)}, f32[4,3,64,128]{3,2,1,0:T(8,128)S(1)}, u32[]{:S(2)}, u32[]{:S(2)}) collective-permute-start(f32[4,3,64,128]{3,2,1,0:T(8,128)S(1)} %pad_maximum_fusion.own), channel_id=1, source_target_pairs={{0,1},{1,0},{2,3},{3,2},{4,5},{5,4},{6,7},{7,6},{8,9},{9,8},{10,11... | collective-permute-start | bytes 1179656 | tf_op jit(solution)/shard_map/ppermute | solution.py:23
  44.7 9.8 %collective-permute-start.11 = (f32[4,64,128]{2,1,0:T(8,128)S(1)}, f32[4,64,128]{2,1,0:T(8,128)S(1)}, u32[]{:S(2)}, u32[]{:S(2)}) collective-permute-start(f32[4,64,128]{2,1,0:T(8,128)S(1)} %pad_maximum_fusion.1), channel_id=1, source_target_pairs={{8,0},{9,1},{10,2},{11,3},{12,4},{13,5},{14,6},{15,7},{16,8},{17,9... | collective-permute-start | bytes 393224 | tf_op jit(solution)/shard_map/ppermute | solution.py:47
  48.0 9.0 %collective-permute-start.15 = (f32[4,64,128]{2,1,0:T(8,128)S(1)}, f32[4,64,128]{2,1,0:T(8,128)S(1)}, u32[]{:S(2)}, u32[]{:S(2)}) collective-permute-start(f32[4,64,128]{2,1,0:T(8,128)S(1)} %pad_maximum_fusion.2), channel_id=1, source_target_pairs={{0,32},{1,33},{2,34},{3,35},{4,36},{5,37},{6,38},{7,39},{8,40},{9,... | collective-permute-start | bytes 393224 | tf_op jit(solution)/shard_map/ppermute | solution.py:23
  54.5 6.8 %collective-permute-start.16 = (f32[4,64,128]{2,1,0:T(8,128)S(1)}, f32[4,64,128]{2,1,0:T(8,128)S(1)}, u32[]{:S(2)}, u32[]{:S(2)}) collective-permute-start(f32[4,64,128]{2,1,0:T(8,128)S(1)} %pad_maximum_fusion.2), channel_id=1, source_target_pairs={{32,0},{33,1},{34,2},{35,3},{36,4},{37,5},{38,6},{39,7},{40,8},{41... | collective-permute-start | bytes 393224 | tf_op jit(solution)/shard_map/ppermute | solution.py:23
  57.0 6.4 %copy-start.7 = (f32[12,64,128]{2,1,0:T(8,128)}, f32[12,64,128]{2,1,0:T(8,128)S(1)}, u32[]{:S(2)}) copy-start(f32[12,64,128]{2,1,0:T(8,128)S(1)} %constant_dynamic-update-slice_fusion.one) | copy-start | bytes 1179652
  61.4 2.0 %copy-start.8 = (f32[12,64,128]{2,1,0:T(8,128)}, f32[12,64,128]{2,1,0:T(8,128)S(1)}, u32[]{:S(2)}) copy-start(f32[12,64,128]{2,1,0:T(8,128)S(1)} %constant_dynamic-update-slice_fusion.6.two) | copy-start | bytes 1179652
  61.4 0.8 copy-start.9
  67.1 4.0 %collective-permute-start.17 = (f32[64,128]{1,0:T(8,128)S(1)}, f32[64,128]{1,0:T(8,128)S(1)}, u32[]{:S(2)}, u32[]{:S(2)}) collective-permute-start(f32[64,128]{1,0:T(8,128)S(1)} %get-tuple-element.18), channel_id=1, source_target_pairs={{0,6},{1,7},{2,0},{3,1},{4,2},{5,3},{6,4},{7,5},{8,14},{9,15},{10,... | collective-permute-start | bytes 98312 | tf_op jit(solution)/shard_map/ppermute | solution.py:23
  68.3 6.9 %collective-permute-start.18 = (f32[64,128]{1,0:T(8,128)S(1)}, f32[64,128]{1,0:T(8,128)S(1)}, u32[]{:S(2)}, u32[]{:S(2)}) collective-permute-start(f32[64,128]{1,0:T(8,128)S(1)} %get-tuple-element.17), channel_id=1, source_target_pairs={{0,4},{1,5},{2,6},{3,7},{4,0},{5,1},{6,2},{7,3},{8,12},{9,13},{10,... | collective-permute-start | bytes 98312 | tf_op jit(solution)/shard_map/ppermute | solution.py:23
  68.3 12.6 %collective-permute-start.19 = (f32[64,128]{1,0:T(8,128)S(1)}, f32[64,128]{1,0:T(8,128)S(1)}, u32[]{:S(2)}, u32[]{:S(2)}) collective-permute-start(f32[64,128]{1,0:T(8,128)S(1)} %get-tuple-element.16), channel_id=1, source_target_pairs={{0,2},{1,3},{2,4},{3,5},{4,6},{5,7},{6,0},{7,1},{8,10},{9,11},{10,... | collective-permute-start | bytes 98312 | tf_op jit(solution)/shard_map/ppermute | solution.py:23
  71.1 46.6 %collective-permute-start.22 = (f32[1024,256]{1,0:T(8,128)}, f32[1024,256]{1,0:T(8,128)S(1)}, u32[]{:S(2)}, u32[]{:S(2)}) collective-permute-start(f32[1024,256]{1,0:T(8,128)} %get-tuple-element.11), channel_id=1, source_target_pairs={{1,2},{2,1},{3,4},{4,3},{5,6},{6,5},{7,8},{8,7},{9,10},{10,9},{11,... | collective-permute-start | bytes 3145736 | tf_op jit(solution)/shard_map/ppermute | solution.py:53
  75.2 53.7 %collective-permute-start.21 = (f32[1024,256]{1,0:T(8,128)}, f32[1024,256]{1,0:T(8,128)}, u32[]{:S(2)}, u32[]{:S(2)}) collective-permute-start(f32[1024,256]{1,0:T(8,128)} %get-tuple-element.12), channel_id=1, source_target_pairs={{1,2},{2,1},{3,4},{4,3},{5,6},{6,5},{7,8},{8,7},{9,10},{10,9},{11,... | collective-permute-start | bytes 3145736 | tf_op jit(solution)/shard_map/ppermute | solution.py:53
  80.9 4.2 %collective-permute-start.20 = (f32[4,64,128]{2,1,0:T(8,128)S(1)}, f32[4,64,128]{2,1,0:T(8,128)S(1)}, u32[]{:S(2)}, u32[]{:S(2)}) collective-permute-start(f32[4,64,128]{2,1,0:T(8,128)S(1)} %pad_maximum_fusion.3), channel_id=1, source_target_pairs={{0,1},{1,0},{2,3},{3,2},{4,5},{5,4},{6,7},{7,6},{8,9},{9,8},{10,11... | collective-permute-start | bytes 393224 | tf_op jit(solution)/shard_map/ppermute | solution.py:23
  81.0 27.6 %collective-permute-start.23 = (f32[1024,128]{1,0:T(8,128)}, f32[1024,128]{1,0:T(8,128)}, u32[]{:S(2)}, u32[]{:S(2)}) collective-permute-start(f32[1024,128]{1,0:T(8,128)} %get-tuple-element.10), channel_id=1, source_target_pairs={{1,2},{2,1},{3,4},{4,3},{5,6},{6,5},{7,8},{8,7},{9,10},{10,9},{11,... | collective-permute-start | bytes 1572872 | tf_op jit(solution)/shard_map/ppermute | solution.py:53
  85.2 54.1 %collective-permute-start.1 = (f32[1024,256]{1,0:T(8,128)}, f32[1024,256]{1,0:T(8,128)}, u32[]{:S(2)}, u32[]{:S(2)}) collective-permute-start(f32[1024,256]{1,0:T(8,128)} %get-tuple-element.13), channel_id=1, source_target_pairs={{1,2},{2,1},{3,4},{4,3},{5,6},{6,5},{7,8},{8,7},{9,10},{10,9},{11,... | collective-permute-start | bytes 3145736 | tf_op jit(solution)/shard_map/ppermute | solution.py:53
  91.1 0.7 copy-start.3
  117.7 1.0 copy-start.6

commit v2 on v0

v2 whole, which is shorter than its diff:
```python
import functools

import jax
import jax.numpy as jnp
from jax import lax
from jax.experimental import pallas as pl
from jax.experimental.pallas import tpu as pltpu
from jax.sharding import PartitionSpec as P


LANES = 128
SIDE = 4
CHUNKS = ((0, 3), (3, 2), (5, 3))
RINGS = 2


def permuted(shard, target):
    pairs = []
    for i in range(lax.axis_size("leaf")):
        x, y, z, core = i // 32, i // 8 % 4, i // 2 % 4, i % 2
        to = target(x, y, z, core)
        if to is not None:
            pairs.append((i, ((to[0] * 4 + to[1]) * 4 + to[2]) * 2 + to[3]))
    return lax.ppermute(shard, "leaf", pairs)


def chip_swap(shard):
    return permuted(shard, lambda x, y, z, core: (x, y, z, 1 - core))


def along_z(shard, by):
    return permuted(shard, lambda x, y, z, core: (x, y, (z + by) % 4, core))


def along_y(shard, by):
    return permuted(shard, lambda x, y, z, core: (x, (y + by) % 4, z, core))


def along_x(shard, by):
    return permuted(
        shard, lambda x, y, z, core: (x + by, y, z, core) if 0 <= x + by < 4 else None
    )


def across_chips(shard):
    peers = lax.axis_size("leaf")
    pairs = [(i, i + 1 if i % 2 else i - 1) for i in range(1, peers - 1)]
    return lax.ppermute(shard, "leaf", pairs)


def round_line(shard):
    return permuted(
        shard,
        lambda x, y, z, core: (x, y, (z + 1) % 4, 0) if core else (x, y, (z - 1) % 4, 1),
    )


def relayed(shard):
    pairs = [(i, i + 8) for i in range(0, lax.axis_size("leaf") - 8, 8)]
    pairs += [(i + 15, i + 7) for i, _ in pairs]
    return lax.ppermute(shard, "leaf", pairs)


def ahead(shard):
    return permuted(shard, lambda x, y, z, core: (x, y, (z + 1 - 2 * core) % 4, core))


def opposite(shard):
    return permuted(
        shard, lambda x, y, z, core: (x, y, (z + 2) % 4, core) if core == z % 2 else None
    )


def split(value):
    high = value.astype(jnp.bfloat16)
    low = (value - high.astype(jnp.float32)).astype(jnp.bfloat16)
    return high, low


def dot(a, b):
    return jnp.dot(a, b, preferred_element_type=jnp.float32)


def dot3(a, b):
    a_high, a_low = split(a)
    b_high, b_low = split(b)
    return dot(a_high, b_high) + (dot(a_high, b_low) + dot(a_low, b_high))


VMEM = pl.BlockSpec(memory_space=pltpu.VMEM)
ANY = pl.BlockSpec(memory_space=pl.ANY)
SMEM = pl.BlockSpec(memory_space=pltpu.SMEM)
HBM = pl.BlockSpec(memory_space=pltpu.HBM)
F32 = jnp.float32


def shape(*dims, dtype=F32):
    return jax.ShapeDtypeStruct(dims, dtype)


def place(device):
    number = device[0]
    line = number // 8
    return number % 2, number // 2 % 4, line, line % 4, line // 4


def leaf_kernel(
    device, pairs_one, pairs_two, probes, basis, transfer, couple_one, couple_two, clusters,
    mine, theirs, couplings, around, wide, high, low, *rest,
):
    slices, (basis_in, transfer_in, couple_in, part, sems, small) = rest[:-6], rest[-6:]
    core, z, line, _, _ = place(device)

    def start(source, target, sem):
        copy = pltpu.make_async_copy(source, target, sem)
        copy.start()
        return copy

    little = [start(basis, basis_in, small.at[0]), start(transfer, transfer_in, small.at[1])]
    copies = []
    for (at, width), ref, i in zip(CHUNKS, slices, range(len(CHUNKS))):
        source = probes.at[:, pl.ds(at * LANES, width * LANES)]
        copies.append(start(source, ref, sems.at[i]))
    later = [
        start(couple_one, couple_in.at[pl.ds(0, 4)], small.at[2]),
        start(couple_two, couple_in.at[pl.ds(4, 1)], small.at[3]),
    ]
    for j in range(SIDE):
        cluster = line * 4 + (z + j) % 4
        later.append(start(clusters.at[cluster], around.at[j], small.at[4 + j]))
    for copy in little:
        copy.wait()
    rows = [dot3(transfer_in[leaf].T, basis_in[leaf]) for leaf in range(2)]
    across = jnp.concatenate(rows, axis=1)
    w_high, w_low = split(across.T)
    wide[...] = jnp.concatenate([w_high, w_low, w_high], axis=1)
    w_high, w_low = split(across)
    w_both = jnp.concatenate([w_high, w_low], axis=0)
    for copy in later:
        copy.wait()
    couplings[0] = jnp.concatenate([couple_in[0], couple_in[1]], axis=1)
    couplings[1] = jnp.concatenate([couple_in[2], couple_in[3]], axis=1)
    lane = lax.broadcasted_iota(jnp.int32, (64, 64), 1)
    ids = jnp.zeros((64, 64), F32)
    for i in range(5):
        value = pairs_one[i] if i < 4 else pairs_two[0]
        ids = jnp.where(lane == i, value.astype(F32), ids)
    couplings[2] = jnp.concatenate([couple_in[4], ids], axis=1)
    for (at, width), ref, copy in zip(CHUNKS, slices, copies):
        copy.wait()
        cols = pl.ds(at * LANES, width * LANES)
        a, b = split(ref[...])
        high[:, cols] = a
        low[:, cols] = b
        terms = dot(w_both, a)
        part[:, cols] = terms[:64] + (terms[64:] + dot(w_high, b))
    mine[...] = part[:, pl.ds(pl.multiple_of(core * 512, 512), 512)]
    theirs[...] = part[:, pl.ds(pl.multiple_of((1 - core) * 512, 512), 512)]


def leaf_stage(device, pairs_one, pairs_two, *arrays):
    bf16 = jnp.bfloat16
    shapes = [shape(64, 512), shape(64, 512), shape(3, 64, LANES), shape(4, 64, 64)]
    shapes += [shape(1024, 192, dtype=bf16), shape(1024, 1024, dtype=bf16), shape(1024, 1024, dtype=bf16)]
    shapes += [shape(1024, width * LANES) for _, width in CHUNKS]
    return pl.pallas_call(
        leaf_kernel,
        out_shape=shapes,
        in_specs=[SMEM] * 3 + [HBM] * 6,
        out_specs=[VMEM] * len(shapes),
        scratch_shapes=[
            pltpu.VMEM((2, 64, 512), F32),
            pltpu.VMEM((2, 64, 64), F32),
            pltpu.VMEM((5, 64, 64), F32),
            pltpu.VMEM((64, 1024), F32),
            pltpu.SemaphoreType.DMA((len(CHUNKS),)),
            pltpu.SemaphoreType.DMA((8,)),
        ],
        compiler_params=pltpu.CompilerParams(vmem_limit_bytes=12 << 20),
        cost_estimate=pl.CostEstimate(
            flops=400_000_000, bytes_accessed=8_000_000, transcendentals=0
        ),
        name="leaf_stage",
    )(
        device,
        pairs_one,
        pairs_two,
        *[pltpu.with_memory_space_constraint(a, pltpu.HBM) for a in arrays],
    )


def small_call(kernel, outs, *args, scalars=1, scratch=()):
    return pl.pallas_call(
        kernel,
        out_shape=outs,
        in_specs=[SMEM] * scalars + [VMEM] * (len(args) - scalars),
        out_specs=[VMEM] * len(outs),
        scratch_shapes=list(scratch),
        compiler_params=pltpu.CompilerParams(vmem_limit_bytes=10 << 20),
        cost_estimate=pl.CostEstimate(
            flops=10_000_000, bytes_accessed=1_000_000, transcendentals=0
        ),
    )(*args)


def cut_kernel(device, mine, got, *pieces):
    _, z, _, _, _ = place(device)
    for j, piece in enumerate(pieces):
        cols = pl.ds(pl.multiple_of((z + j) % 4 * LANES, LANES), LANES)
        piece[...] = mine[:, cols] + got[:, cols]


def lift_kernel(device, first, second, third, fourth, around, level, coef):
    total = jnp.zeros((64, LANES), F32)
    for j, ref in enumerate((first, second, third, fourth)):
        value = ref[...]
        level[j] = value
        total += dot3(around[j].T, value)
    level[4] = total
    coef[...] = total


def plane_kernel(device, level, below, across, above, plane, from_below, from_above):
    plane[0] = level[4]
    plane[1] = above[4]
    plane[2] = across[...]
    plane[3] = below[4]
    for target, source in ((from_below, below), (from_above, above)):
        target[pl.ds(0, 4)] = plane[...]
        target[pl.ds(4, 4)] = source[pl.ds(0, 4)]


def far_kernel(device, count_one, count_two, *refs):
    level, below, above, plane, before, after, own, other, around = refs[:9]
    down, one, two, ids, sems = refs[9:]
    core, z, line, y, x = place(device)
    tables = (own, other)
    copies = []
    for side in range(2):
        for j in range(SIDE):
            i = side * 4 + j
            source = tables[side].at[j, 2, pl.ds(0, 8), :]
            copies.append(pltpu.make_async_copy(source, ids.at[i], sems.at[i]))
            copies[-1].start()
    one[pl.ds(4, 4)] = level[pl.ds(0, 4)]
    one[pl.ds(0, 4)] = jnp.where(y == 0, before[pl.ds(4, 4)], below[pl.ds(0, 4)])
    one[pl.ds(8, 4)] = jnp.where(y == 3, after[pl.ds(4, 4)], above[pl.ds(0, 4)])
    two[pl.ds(0, 4)] = before[pl.ds(0, 4)]
    two[pl.ds(4, 4)] = plane[...]
    two[pl.ds(8, 4)] = after[pl.ds(0, 4)]
    for copy in copies:
        copy.wait()

    def partner(side, j, s):
        return ids[side * 4 + j, 0, 64 + s].astype(jnp.int32)

    def kept(value, keep):
        return jnp.where(keep, value, jnp.zeros_like(value))

    far_two = jnp.zeros((64, LANES), F32)
    for side in range(2):
        left, right = [], []
        for j in range(SIDE):
            left.append(tables[side][j, 2][:, :64])
            p = partner(side, j, 4)
            slot = (z + j) % 4 * 2 + (core if side == 0 else 1 - core)
            at = jnp.clip((p // 4 - x + 1) * 4 + (p % 4 - y + 4) % 4, 0, 11)
            right.append(kept(two[at], slot < count_two[line]))
        far_two += dot3(jnp.concatenate(left, axis=1), jnp.concatenate(right, axis=0))
    for j in range(SIDE):
        total = dot3(around[j], far_two)
        count = count_one[line * 4 + (z + j) % 4]
        for side in range(2):
            left = jnp.concatenate([tables[side][j, 0], tables[side][j, 1]], axis=1)
            right = []
            for s in range(4):
                p = partner(side, j, s)
                slot = (core if side == 0 else 1 - core) * 4 + s
                at = jnp.clip((p // 4 - line + 1) * 4 + (p % 4 - z + 4) % 4, 0, 11)
                right.append(kept(one[at], slot < count))
            total += dot3(left, jnp.concatenate(right, axis=0))
        down[j] = total


def pack_kernel(device, down, other, first, second):
    core, _, _, _, _ = place(device)
    for side in range(2):
        for target, j in ((first, 1 + 2 * core), (second, 2)):
            target[side] = jnp.where(core == side, down[j], other[j])


def unpack_kernel(device, down, other, back, other_back, table):
    core, z, _, _, _ = place(device)

    def got(on, kind, side):
        return jnp.where(core == on, back[kind, side], other_back[kind, side])

    def put(side, chip, value):
        cols = pl.ds(pl.multiple_of((side * 4 + chip) * LANES, LANES), LANES)
        high, low = split(value)
        table[:, cols] = jnp.concatenate([high, high, low], axis=0)

    for side in range(2):
        put(side, z, jnp.where(core == side, down[0], other[0]))
        put(side, (z + 1) % 4, got(1, 0, side))
        put(side, (z + 2) % 4, got(z % 2, 1, side))
        put(side, (z + 3) % 4, got(0, 0, side))


def block_kernel(blocks, high, low):
    for i in range(6):
        high[i], low[i] = split(blocks[i // 3, i % 3])


def block_stage(near_blocks):
    half = shape(6, 512, 512, dtype=jnp.bfloat16)
    return small_call(block_kernel, [half, half], near_blocks, scalars=0)


def near_kernel(at, width, at_old, last, device, near_list, *refs):
    n_high, n_low, p_high, p_low, chip, wide, table, cross, relay = refs[:9]
    both, sems = refs[-2:]
    old = (at_old, refs[9]) if at_old is not None else None
    if last:
        out, buffer = refs[-4], refs[-3]
    else:
        out, buffer = (refs[-4] if old else None), refs[-3]
    core, z, _, _, _ = place(device)
    span = width * LANES
    cols = pl.ds(at * LANES, span)
    high, low = pl.ds(0, span), pl.ds(span, span)
    for i in range(2):
        rows = pl.ds(i * 512, 512)
        both[i, :, high], both[i, :, low] = p_high[rows, cols], p_low[rows, cols]
        both[2 + i, :, high], both[2 + i, :, low] = split(chip[rows, cols])
        beside = cross[rows, :]
        if at < CHUNKS[RINGS][0]:
            beside = jnp.where(z == 3 * core, relay[rows, :], beside)
        both[4 + i, :, high], both[4 + i, :, low] = split(beside)
    copies = []
    if old:
        (at_old, buffer_old) = old
        copies.append(
            pltpu.make_async_copy(
                buffer_old, out.at[:, pl.ds(at_old * LANES, buffer_old.shape[1])], sems.at[2]
            )
        )
        copies[-1].start()
    for leaf in range(2):
        rows = pl.ds(leaf * 512, 512)
        total = dot(wide[rows, :], table[:, cols])
        for m in range(3):
            i = leaf * 3 + m
            local = near_list[leaf, m] - 2 * device[0]
            before = jnp.where(core == 0, 4, 2) + local + 2
            after = jnp.where(core == 0, 2, 4) + local - 2
            slot = jnp.where(local < 0, before, jnp.where(local > 1, after, local))
            wide_terms = dot(n_high[i], both[slot])
            total += wide_terms[:, :span]
            total += wide_terms[:, span:]
            total += dot(n_low[i], both[slot, :, high])
        buffer[rows, :] = total
        if last:
            copies.append(
                pltpu.make_async_copy(buffer.at[rows], out.at[rows, cols], sems.at[leaf])
            )
            copies[-1].start()
    for copy in copies:
        copy.wait()


def near_field(chunk, device, near_list, arrays, old, out):
    (at, width), last = CHUNKS[chunk], chunk == len(CHUNKS) - 1
    cols = width * LANES
    at_old = CHUNKS[chunk - 1][0] if chunk else None
    args = [device, near_list, *arrays]
    in_specs = [SMEM] * 2 + [VMEM] * len(arrays)
    aliases = {}
    if chunk:
        args.append(old)
        in_specs.append(VMEM)
    if out is not None:
        in_specs.append(ANY)
        aliases = {len(args): 0}
        args.append(out)
    shapes, out_specs = [], []
    if chunk:
        shapes.append(shape(1024, 1024))
        out_specs.append(ANY)
    scratch = []
    if last:
        scratch.append(pltpu.VMEM((1024, cols), F32))
    else:
        shapes.append(shape(1024, cols))
        out_specs.append(VMEM)
    scratch.append(pltpu.VMEM((6, 512, 2 * cols), jnp.bfloat16))
    scratch.append(pltpu.SemaphoreType.DMA((3,)))
    results = pl.pallas_call(
        functools.partial(near_kernel, at, width, at_old, last),
        out_shape=shapes,
        in_specs=in_specs,
        out_specs=out_specs,
        scratch_shapes=scratch,
        input_output_aliases=aliases,
        compiler_params=pltpu.CompilerParams(vmem_limit_bytes=16 << 20),
        cost_estimate=pl.CostEstimate(
            flops=1_250_000_000 * width, bytes_accessed=2_000_000, transcendentals=0
        ),
        name="near_field",
    )(*args)
    return (results[0] if chunk else None), (None if last else results[-1])


def body(
    probes,
    leaf_basis,
    leaf_transfer,
    cluster_transfer,
    couple_one,
    pairs_one,
    count_one,
    couple_two,
    pairs_two,
    count_two,
    near_blocks,
    near_list,
):
    device = lax.axis_index("leaf").reshape(1)

    mine, theirs, couplings, around, wide, p_high, p_low, *slices = leaf_stage(
        device,
        pairs_one,
        pairs_two,
        probes,
        jnp.swapaxes(leaf_basis, 1, 2),
        leaf_transfer,
        couple_one,
        couple_two,
        cluster_transfer,
    )
    crosses, relays = [], []
    for i, piece in enumerate(slices):
        if i < RINGS:
            crosses.append(round_line(piece))
            relays.append(relayed(crosses[i]))
        else:
            crosses.append(across_chips(piece))
            relays.append(crosses[i])

    own_table = jnp.stack(
        [
            couplings,
            along_z(couplings, -1),
            along_z(couplings, 2),
            along_z(couplings, 1),
        ]
    )
    other_table = chip_swap(own_table)

    got = chip_swap(theirs)
    pieces = small_call(cut_kernel, [shape(64, LANES)] * 4, device, mine, got)
    level, coef_two = small_call(
        lift_kernel,
        [shape(5, 64, LANES), shape(64, LANES)],
        device,
        pieces[0],
        along_z(pieces[3], -1),
        along_z(pieces[2], 2),
        along_z(pieces[1], 1),
        around,
    )
    chip = chip_swap(probes)
    blocks = block_stage(near_blocks)

    above = along_y(level, -1)
    across = along_y(coef_two, 2)
    below = along_y(level, 1)
    plane, upward, downward = small_call(
        plane_kernel,
        [shape(4, 64, LANES), shape(8, 64, LANES), shape(8, 64, LANES)],
        device,
        level,
        below,
        across,
        above,
    )
    (down,) = small_call(
        far_kernel,
        [shape(4, 64, LANES)],
        device,
        count_one,
        count_two,
        level,
        below,
        above,
        plane,
        along_x(upward, 1),
        along_x(downward, -1),
        own_table,
        other_table,
        around,
        scalars=3,
        scratch=(
            pltpu.VMEM((12, 64, LANES), F32),
            pltpu.VMEM((12, 64, LANES), F32),
            pltpu.SMEM((8, 8, LANES), F32),
            pltpu.SemaphoreType.DMA((8,)),
        ),
    )
    other = chip_swap(down)
    pair = [shape(2, 64, LANES)] * 2
    first, second = small_call(pack_kernel, pair, device, down, other)
    back = jnp.stack([ahead(first), opposite(second)])
    other_back = chip_swap(back)
    (table,) = small_call(
        unpack_kernel, [shape(192, 1024, dtype=jnp.bfloat16)], device, down, other, back, other_back
    )

    out = old = None
    for i, (cross, relay) in enumerate(zip(crosses, relays)):
        arrays = (*blocks, p_high, p_low, chip, wide, table, cross, relay)
        out, old = near_field(i, device, near_list, arrays, old, out)
    return out


def solution(mesh):
    return jax.shard_map(
        body,
        mesh=mesh,
        in_specs=(
            P("leaf", None),
            P("leaf", None, None),
            P("leaf", None, None),
            P(),
            P("leaf", None, None),
            P("leaf"),
            P(),
            P("leaf", None, None),
            P("leaf"),
            P(),
            P("leaf", None, None, None),
            P("leaf", None),
        ),
        out_specs=P("leaf", None),
        check_vma=False,
    )
```

time: 289 us -> 159 us (0.55); the launches traced: 283 us -> 157 us
  starting transfers between devices: 121 us -> 33.7 us
  matrix products: 46.7 us -> 0 us
  Pallas kernels: 0 us -> 32.2 us
  local copies, waits for them, and re-layouts: 13.2 us -> 0.82 us
  other arithmetic: 8.74 us -> 0.04 us
    ppermute x33 -> x23, starting transfers between devices: 121 us -> 33.7 us  [the longest x20 26.4 us: permuted(): return lax.ppermute(shard, 'leaf', pairs)]
    dot_general x11 -> x0, matrix products: 46.7 us -> none  [the longest x1 26.7 us: body(): jnp.einsum('lmab,lmbp->lap', near_blocks, near_rows, precision=highest)]
    pallas_call x0 -> x11, Pallas kernels: none -> 32.2 us  [the longest x3 23 us: near_field(): pl.pallas_call(functools.partial(near_kernel, at, width, at_old, last), o...]
    gather x3 -> x0, local copies, waits for them, and re-layouts: 12.6 us -> none  [the longest x1 11.4 us: body(): jnp.take(padded, local_index.reshape(-1), axis=0)]
    concatenate x1 -> x0, other arithmetic: 8.52 us -> none  [padded_2(): shard = jnp.concatenate([before, shard, after], axis=dim)]
    ppermute x33 -> x23, waiting for transfers between devices: 91.2 us -> 89.6 us  [the longest x20 89.6 us: permuted(): return lax.ppermute(shard, 'leaf', pairs)]
  transfers between devices with their start and end apart: 33 -> 23, of which waited for: 17 -> 12; matrix products, arithmetic and copies ran while one was open for 8% -> 0% of each run, Pallas kernels for 0% -> 15%
where the time goes in v2:
time: 159 us; the launch traced here: 157 us
  waiting for transfers between devices  89.6 us (56%)
  starting transfers between devices  33.7 us (21%)
  Pallas kernels  32.2 us (20%)
    ppermute x20, waiting for transfers between devices, permuted(): return lax.ppermute(shard, 'leaf', pairs)  89.6 us
    ppermute x20, starting transfers between devices, permuted(): return lax.ppermute(shard, 'leaf', pairs)  26.4 us
    pallas_call x3, Pallas kernels, near_field(): pl.pallas_call(functools.partial(near_kernel, at, width, at_old, last), o...  23 us
    ppermute x2, starting transfers between devices, relayed(): return lax.ppermute(shard, 'leaf', pairs)  5.4 us
    pallas_call x1, Pallas kernels, leaf_stage(): pl.pallas_call(leaf_kernel, out_shape=shapes, in_specs=[SMEM] * 3 + [HBM]...  5.2 us
    pallas_call x7, Pallas kernels, small_call(): pl.pallas_call(kernel, out_shape=outs, in_specs=[SMEM] * scalars + [VMEM]...  3.99 us
  transfers between devices with their start and end apart: 23, of which 12 were waited for; matrix products, arithmetic and copies ran while one was open for 0% of the time, Pallas kernels for 15%

profile of v2, /device:TPU:2, one launch (start us, length us, event | category | flops | bytes accessed | tf_op | source)
XLA Modules:
  0.0 157.4 jit_solution(15926559670294922360)
XLA Ops:
  0.7 0.8 copy-done.1
  1.5 5.2 %leaf_stage.1 = (f32[64,512]{1,0:T(8,128)S(1)}, f32[64,512]{1,0:T(8,128)S(1)}, f32[3,64,128]{2,1,0:T(8,128)S(1)}, f32[4,64,64]{2,1,0:T(8,128)S(1)}, bf16[1024,19...) custom-call(s32[1]{0:T(128)} %bitcast.device, ...), custom_call_target="tpu_custom_call" | custom-call | flops 400000000 | bytes 8000000 | tf_op jit(solution)/shard_map/leaf_stage/pallas_call | solution.py:166
  6.7 4.2 %collective-permute-start.21 = (f32[1024,384]{1,0:T(8,128)S(1)}, f32[1024,384]{1,0:T(8,128)S(1)}, u32[]{:S(2)}, u32[]{:S(2)}) collective-permute-start(f32[1024,384]{1,0:T(8,128)S(1)} %get-tuple-element.52), channel_id=1, source_target_pairs={{0,7},{1,2},{2,1},{3,4},{4,3},{5,6},{6,5},{7,0},{8,15},{9,10},{10,... | collective-permute-start | bytes 4718600 | tf_op jit(solution)/shard_map/ppermute | solution.py:24
  10.9 0.5 collective-permute-start.19
  11.4 1.6 %collective-permute-start.12 = (f32[3,64,128]{2,1,0:T(8,128)S(1)}, f32[3,64,128]{2,1,0:T(8,128)S(1)}, u32[]{:S(2)}, u32[]{:S(2)}) collective-permute-start(f32[3,64,128]{2,1,0:T(8,128)S(1)} %get-tuple-element.47), channel_id=1, source_target_pairs={{0,2},{1,3},{2,4},{3,5},{4,6},{5,7},{6,0},{7,1},{8,10},{9,11},{10,... | collective-permute-start | bytes 294920 | tf_op jit(solution)/shard_map/ppermute | solution.py:24
  13.1 0.0 collective-permute-done.1.got
  13.1 1.7 %collective-permute-start.2 = (f32[64,128]{1,0:T(8,128)S(1)}, f32[64,128]{1,0:T(8,128)S(1)}, u32[]{:S(2)}, u32[]{:S(2)}) collective-permute-start(f32[64,128]{1,0:T(8,128)S(1)} %get-tuple-element.38), channel_id=1, source_target_pairs={{0,6},{1,7},{2,0},{3,1},{4,2},{5,3},{6,4},{7,5},{8,14},{9,15},{10,... | collective-permute-start | bytes 98312 | tf_op jit(solution)/shard_map/ppermute | solution.py:24
  14.8 3.5 %collective-permute-done.12 = f32[3,64,128]{2,1,0:T(8,128)S(1)} collective-permute-done((f32[3,64,128]{2,1,0:T(8,128)S(1)}, f32[3,64,128]{2,1,0:T(8,128)S(1)}, u32[]{:S(2)}, u32[]{:S(2)}) %collective-permute-start.12) | collective-permute-done | bytes 98336 | tf_op jit(solution)/shard_map/ppermute | solution.py:24
  18.3 0.5 collective-permute-start.3
  18.8 22.4 %collective-permute-done.2.second = f32[64,128]{1,0:T(8,128)S(1)} collective-permute-done((f32[64,128]{1,0:T(8,128)S(1)}, f32[64,128]{1,0:T(8,128)S(1)}, u32[]{:S(2)}, u32[]{:S(2)}) %collective-permute-start.2) | collective-permute-done | bytes 32800 | tf_op jit(solution)/shard_map/ppermute | solution.py:24
  41.1 0.0 collective-permute-start.4
  41.1 5.1 %collective-permute-start.11 = (f32[3,64,128]{2,1,0:T(8,128)S(1)}, f32[3,64,128]{2,1,0:T(8,128)S(1)}, u32[]{:S(2)}, u32[]{:S(2)}) collective-permute-start(f32[3,64,128]{2,1,0:T(8,128)S(1)} %get-tuple-element.47), channel_id=1, source_target_pairs={{0,4},{1,5},{2,6},{3,7},{4,0},{5,1},{6,2},{7,3},{8,12},{9,13},{10,... | collective-permute-start | bytes 294920 | tf_op jit(solution)/shard_map/ppermute | solution.py:24
  46.3 0.4 collective-permute-done.4.fourth
  46.7 2.0 %collective-permute-start.10 = (f32[3,64,128]{2,1,0:T(8,128)S(1)}, f32[3,64,128]{2,1,0:T(8,128)S(1)}, u32[]{:S(2)}, u32[]{:S(2)}) collective-permute-start(f32[3,64,128]{2,1,0:T(8,128)S(1)} %get-tuple-element.47), channel_id=1, source_target_pairs={{0,6},{1,7},{2,0},{3,1},{4,2},{5,3},{6,4},{7,5},{8,14},{9,15},{10,... | collective-permute-start | bytes 294920 | tf_op jit(solution)/shard_map/ppermute | solution.py:24
  48.7 3.5 %collective-permute-start.22 = (f32[1024,384]{1,0:T(8,128)S(1)}, f32[1024,384]{1,0:T(8,128)S(1)}, u32[]{:S(2)}, u32[]{:S(2)}) collective-permute-start(f32[1024,384]{1,0:T(8,128)S(1)} %collective-permute-done.21.refs_7_), channel_id=1, source_target_pairs={{0,8},{8,16},{16,24},{24,32},{32,40},{40,48},{48,56},{56,64},{64,7... | collective-permute-start | bytes 4718600 | tf_op jit(solution)/shard_map/ppermute | solution.py:61
  52.2 0.3 shard_map.120
  52.5 0.0 collective-permute-done.11
  52.5 3.0 %collective-permute-start.7 = (f32[64,128]{1,0:T(8,128)S(1)}, f32[64,128]{1,0:T(8,128)S(1)}, u32[]{:S(2)}, u32[]{:S(2)}) collective-permute-start(f32[64,128]{1,0:T(8,128)S(1)} %get-tuple-element.43), channel_id=1, source_target_pairs={{0,16},{1,17},{2,18},{3,19},{4,20},{5,21},{6,22},{7,23},{8,24},{9,... | collective-permute-start | bytes 98312 | tf_op jit(solution)/shard_map/ppermute | solution.py:24
  55.5 0.0 collective-permute-done.10
  55.5 0.1 collective-permute-start.13
  55.6 20.0 %collective-permute-done.7.across = f32[64,128]{1,0:T(8,128)S(1)} collective-permute-done((f32[64,128]{1,0:T(8,128)S(1)}, f32[64,128]{1,0:T(8,128)S(1)}, u32[]{:S(2)}, u32[]{:S(2)}) %collective-permute-start.7) | collective-permute-done | bytes 32800 | tf_op jit(solution)/shard_map/ppermute | solution.py:24
  75.6 5.3 %collective-permute-done.6.above.refs_2_ = f32[5,64,128]{2,1,0:T(8,128)S(1)} collective-permute-done((f32[5,64,128]{2,1,0:T(8,128)S(1)}, f32[5,64,128]{2,1,0:T(8,128)S(1)}, u32[]{:S(2)}, u32[]{:S(2)}) %collective-permute-start.6) | collective-permute-done | bytes 163872 | tf_op jit(solution)/shard_map/ppermute | solution.py:24
  80.9 0.0 collective-permute-start.5
  80.9 6.5 %collective-permute-done.5.below.refs_1_ = f32[5,64,128]{2,1,0:T(8,128)S(1)} collective-permute-done((f32[5,64,128]{2,1,0:T(8,128)S(1)}, f32[5,64,128]{2,1,0:T(8,128)S(1)}, u32[]{:S(2)}, u32[]{:S(2)}) %collective-permute-start.5) | collective-permute-done | bytes 163872 | tf_op jit(solution)/shard_map/ppermute | solution.py:24
  87.5 3.4 %collective-permute-start.8 = (f32[8,64,128]{2,1,0:T(8,128)S(1)}, f32[8,64,128]{2,1,0:T(8,128)S(1)}, u32[]{:S(2)}, u32[]{:S(2)}) collective-permute-start(f32[8,64,128]{2,1,0:T(8,128)S(1)} %get-tuple-element.45), channel_id=1, source_target_pairs={{0,32},{1,33},{2,34},{3,35},{4,36},{5,37},{6,38},{7,39},{8,40},{9,... | collective-permute-start | bytes 786440 | tf_op jit(solution)/shard_map/ppermute | solution.py:24
  90.9 0.0 collective-permute-done.13.refs_7_
  90.9 1.9 %collective-permute-start.18 = (f32[1024,384]{1,0:T(8,128)S(1)}, f32[1024,384]{1,0:T(8,128)S(1)}, u32[]{:S(2)}, u32[]{:S(2)}) collective-permute-start(f32[1024,384]{1,0:T(8,128)S(1)} %get-tuple-element.50), channel_id=1, source_target_pairs={{1,2},{2,1},{3,4},{4,3},{5,6},{6,5},{7,8},{8,7},{9,10},{10,9},{11,... | collective-permute-start | bytes 4718600 | tf_op jit(solution)/shard_map/ppermute | solution.py:48
  92.8 2.9 %collective-permute-done.8.refs_4_ = f32[8,64,128]{2,1,0:T(8,128)S(1)} collective-permute-done((f32[8,64,128]{2,1,0:T(8,128)S(1)}, f32[8,64,128]{2,1,0:T(8,128)S(1)}, u32[]{:S(2)}, u32[]{:S(2)}) %collective-permute-start.8) | collective-permute-done | bytes 262176 | tf_op jit(solution)/shard_map/ppermute | solution.py:24
  95.8 1.9 %collective-permute-start.9 = (f32[8,64,128]{2,1,0:T(8,128)S(1)}, f32[8,64,128]{2,1,0:T(8,128)S(1)}, u32[]{:S(2)}, u32[]{:S(2)}) collective-permute-start(f32[8,64,128]{2,1,0:T(8,128)S(1)} %get-tuple-element.46), channel_id=1, source_target_pairs={{32,0},{33,1},{34,2},{35,3},{36,4},{37,5},{38,6},{39,7},{40,8},{41... | collective-permute-start | bytes 786440 | tf_op jit(solution)/shard_map/ppermute | solution.py:24
  97.7 1.9 %collective-permute-start.20 = (f32[1024,256]{1,0:T(8,128)S(1)}, f32[1024,256]{1,0:T(8,128)S(1)}, u32[]{:S(2)}, u32[]{:S(2)}) collective-permute-start(f32[1024,256]{1,0:T(8,128)S(1)} %collective-permute-done.19.refs_7_), channel_id=1, source_target_pairs={{0,8},{8,16},{16,24},{24,32},{32,40},{40,48},{48,56},{56,64},{64,7... | collective-permute-start | bytes 3145736 | tf_op jit(solution)/shard_map/ppermute | solution.py:61
  99.6 15.6 %collective-permute-done.9.refs_5_ = f32[8,64,128]{2,1,0:T(8,128)S(1)} collective-permute-done((f32[8,64,128]{2,1,0:T(8,128)S(1)}, f32[8,64,128]{2,1,0:T(8,128)S(1)}, u32[]{:S(2)}, u32[]{:S(2)}) %collective-permute-start.9) | collective-permute-done | bytes 262176 | tf_op jit(solution)/shard_map/ppermute | solution.py:24
  115.2 2.6 %shard_map.122.down = f32[4,64,128]{2,1,0:T(8,128)S(1)} custom-call(s32[1]{0:T(128)} %bitcast.device, s32[64]{0:T(128)S(1)} %copy-done.2, s32[16]{0:T(128)S(1)} %copy-done.3, f32[5,64,128]{2,1,0:T(8,128)S(1)} %get-tuple-element.42.level.refs_0_, f32[5,64,128]{2,1,0:T(8,128)S(1)} %collective-permute-done.5.below.refs_1_, ...), custom_call_target="tpu_custom_call" | custom-call | flops 10000000 | bytes 1000000 | tf_op jit(solution)/shard_map/pallas_call | solution.py:193
  117.8 0.1 collective-permute-start.14
  117.9 1.3 collective-permute-done.14.other
  119.2 0.1 collective-permute-start.15
  119.3 5.5 %collective-permute-done.15 = f32[2,64,128]{2,1,0:T(8,128)S(1)} collective-permute-done((f32[2,64,128]{2,1,0:T(8,128)S(1)}, f32[2,64,128]{2,1,0:T(8,128)S(1)}, u32[]{:S(2)}, u32[]{:S(2)}) %collective-permute-start.15) | collective-permute-done | bytes 65568 | tf_op jit(solution)/shard_map/ppermute | solution.py:24
  124.8 1.9 %collective-permute-start.16 = (f32[2,64,128]{2,1,0:T(8,128)S(1)}, f32[2,64,128]{2,1,0:T(8,128)S(1)}, u32[]{:S(2)}, u32[]{:S(2)}) collective-permute-start(f32[2,64,128]{2,1,0:T(8,128)S(1)} %get-tuple-element.49), channel_id=1, source_target_pairs={{0,4},{3,7},{4,0},{7,3},{8,12},{11,15},{12,8},{15,11},{16,20},{19,... | collective-permute-start | bytes 196616 | tf_op jit(solution)/shard_map/ppermute | solution.py:24
  126.7 5.7 %collective-permute-done.16 = f32[2,64,128]{2,1,0:T(8,128)S(1)} collective-permute-done((f32[2,64,128]{2,1,0:T(8,128)S(1)}, f32[2,64,128]{2,1,0:T(8,128)S(1)}, u32[]{:S(2)}, u32[]{:S(2)}) %collective-permute-start.16) | collective-permute-done | bytes 65568 | tf_op jit(solution)/shard_map/ppermute | solution.py:24
  132.5 0.0 copy-start
  132.5 0.3 collective-permute-start.17
  132.8 1.0 shard_map.118
  133.7 0.3 collective-permute-done.17.other_back
  134.1 0.1 shard_map.124.refs_6_
  134.2 0.0 collective-permute-done.22.refs_8_
  134.2 0.0 collective-permute-done.refs_4_
  134.2 7.9 %near_field.3.refs_9_ = f32[1024,384]{1,0:T(8,128)S(1)} custom-call(s32[1]{0:T(128)} %bitcast.device, s32[2,3]{1,0:T(2,128)S(1)} %copy-done, bf16[6,512,512]{2,1,0:T(8,128)(2,1)S(1)} %get-tuple-element.30.refs_0_, bf16[6,512,512]{2,1,0:T(8,128)(2,1)S(1)} %get-tuple-element.31.refs_1_, bf16[1024,1024]{1,0:T(8,128)(2,1)S(1)} %get-tuple-element.32.refs_2_, ...), custom_call_target="tpu_custom_call" | custom-call | flops 3750000128 | bytes 2000000 | tf_op jit(solution)/shard_map/near_field/pallas_call | solution.py:398
  142.1 6.4 %near_field.4 = (f32[1024,1024]{1,0:T(8,128)}, f32[1024,256]{1,0:T(8,128)S(1)}) custom-call(s32[1]{0:T(128)} %bitcast.device, s32[2,3]{1,0:T(2,128)S(1)} %copy-done, bf16[6,512,512]{2,1,0:T(8,128)(2,1)S(1)} %get-tuple-element.30.refs_0_, bf16[6,512,512]{2,1,0:T(8,128)(2,1)S(1)} %get-tuple-element.31.refs_1_, ...), custom_call_target="tpu_custom_call" | custom-call | flops 2500000000 | bytes 2000000 | tf_op jit(solution)/shard_map/near_field/pallas_call | solution.py:398
  148.6 8.7 %near_field.5 = f32[1024,1024]{1,0:T(8,128)} custom-call(s32[1]{0:T(128)} %bitcast.device, s32[2,3]{1,0:T(2,128)S(1)} %copy-done, bf16[6,512,512]{2,1,0:T(8,128)(2,1)S(1)} %get-tuple-element.30.refs_0_, bf16[6,512,512]{2,1,0:T(8,128)(2,1)S(1)} %get-tuple-element.31.refs_1_, ...), custom_call_target="tpu_custom_call", output_to_operand_aliasing={{}: (12, {})} | custom-call | flops 3750000128 | bytes 2000000 | tf_op jit(solution)/shard_map/near_field/pallas_call | solution.py:398
  (24 shorter events, 0.2 us)
Async XLA Ops:
  0.0 134.2 %collective-permute-start = (f32[1024,1024]{1,0:T(8,128)}, f32[1024,1024]{1,0:T(8,128)}, u32[]{:S(2)}, u32[]{:S(2)}) collective-permute-start(f32[1024,1024]{1,0:T(8,128)} %probes.1), channel_id=1, source_target_pairs={{0,1},{1,0},{2,3},{3,2},{4,5},{5,4},{6,7},{7,6},{8,9},{9,8},{10,11... | collective-permute-start | bytes 12582920 | tf_op jit(solution)/shard_map/ppermute | solution.py:24
  0.7 132.1 %slice-start = ((s8[6291456]{0:T(1024)(128)(4,1)}), s8[4194304]{0:T(1024)(128)(4,1)S(1)}, s32[]{:S(2)}) async-start(s8[6291456]{0:T(1024)(128)(4,1)} %bitcast.8), calls=%async_computation | async-start | bytes 8388608
  0.7 0.8 copy-start.1
  1.5 113.8 %copy-start.2 = (s32[64]{0:T(128)S(1)}, s32[64]{0:T(128)}, u32[]{:S(2)}) copy-start(s32[64]{0:T(128)} %count_one.1) | copy-start | bytes 772
  1.5 113.8 %copy-start.3 = (s32[16]{0:T(128)S(1)}, s32[16]{0:T(128)}, u32[]{:S(2)}) copy-start(s32[16]{0:T(128)} %count_two.1) | copy-start | bytes 196
  1.5 131.3 %slice-start.1 = ((s8[6291456]{0:T(1024)(128)(4,1)}), s8[2097152]{0:T(1024)(128)(4,1)S(1)}, s32[]{:S(2)}) async-start(s8[6291456]{0:T(1024)(128)(4,1)} %bitcast.8), calls=%async_computation.1 | async-start | bytes 4194304
  6.7 42.1 %collective-permute-start.21 = (f32[1024,384]{1,0:T(8,128)S(1)}, f32[1024,384]{1,0:T(8,128)S(1)}, u32[]{:S(2)}, u32[]{:S(2)}) collective-permute-start(f32[1024,384]{1,0:T(8,128)S(1)} %get-tuple-element.52), channel_id=1, source_target_pairs={{0,7},{1,2},{2,1},{3,4},{4,3},{5,6},{6,5},{7,0},{8,15},{9,10},{10,... | collective-permute-start | bytes 4718600 | tf_op jit(solution)/shard_map/ppermute | solution.py:24
  10.9 2.1 %collective-permute-start.1 = (f32[64,512]{1,0:T(8,128)S(1)}, f32[64,512]{1,0:T(8,128)S(1)}, u32[]{:S(2)}, u32[]{:S(2)}) collective-permute-start(f32[64,512]{1,0:T(8,128)S(1)} %get-tuple-element.36), channel_id=1, source_target_pairs={{0,1},{1,0},{2,3},{3,2},{4,5},{5,4},{6,7},{7,6},{8,9},{9,8},{10,11... | collective-permute-start | bytes 393224 | tf_op jit(solution)/shard_map/ppermute | solution.py:24
  10.9 86.8 %collective-permute-start.19 = (f32[1024,256]{1,0:T(8,128)S(1)}, f32[1024,256]{1,0:T(8,128)S(1)}, u32[]{:S(2)}, u32[]{:S(2)}) collective-permute-start(f32[1024,256]{1,0:T(8,128)S(1)} %get-tuple-element.51), channel_id=1, source_target_pairs={{0,7},{1,2},{2,1},{3,4},{4,3},{5,6},{6,5},{7,0},{8,15},{9,10},{10,... | collective-permute-start | bytes 3145736 | tf_op jit(solution)/shard_map/ppermute | solution.py:24
  11.4 6.9 %collective-permute-start.12 = (f32[3,64,128]{2,1,0:T(8,128)S(1)}, f32[3,64,128]{2,1,0:T(8,128)S(1)}, u32[]{:S(2)}, u32[]{:S(2)}) collective-permute-start(f32[3,64,128]{2,1,0:T(8,128)S(1)} %get-tuple-element.47), channel_id=1, source_target_pairs={{0,2},{1,3},{2,4},{3,5},{4,6},{5,7},{6,0},{7,1},{8,10},{9,11},{10,... | collective-permute-start | bytes 294920 | tf_op jit(solution)/shard_map/ppermute | solution.py:24
  13.1 28.0 %collective-permute-start.2 = (f32[64,128]{1,0:T(8,128)S(1)}, f32[64,128]{1,0:T(8,128)S(1)}, u32[]{:S(2)}, u32[]{:S(2)}) collective-permute-start(f32[64,128]{1,0:T(8,128)S(1)} %get-tuple-element.38), channel_id=1, source_target_pairs={{0,6},{1,7},{2,0},{3,1},{4,2},{5,3},{6,4},{7,5},{8,14},{9,15},{10,... | collective-permute-start | bytes 98312 | tf_op jit(solution)/shard_map/ppermute | solution.py:24
  18.3 22.8 %collective-permute-start.3 = (f32[64,128]{1,0:T(8,128)S(1)}, f32[64,128]{1,0:T(8,128)S(1)}, u32[]{:S(2)}, u32[]{:S(2)}) collective-permute-start(f32[64,128]{1,0:T(8,128)S(1)} %get-tuple-element.39), channel_id=1, source_target_pairs={{0,4},{1,5},{2,6},{3,7},{4,0},{5,1},{6,2},{7,3},{8,12},{9,13},{10,... | collective-permute-start | bytes 98312 | tf_op jit(solution)/shard_map/ppermute | solution.py:24
  41.1 5.6 %collective-permute-start.4 = (f32[64,128]{1,0:T(8,128)S(1)}, f32[64,128]{1,0:T(8,128)S(1)}, u32[]{:S(2)}, u32[]{:S(2)}) collective-permute-start(f32[64,128]{1,0:T(8,128)S(1)} %get-tuple-element.40), channel_id=1, source_target_pairs={{0,2},{1,3},{2,4},{3,5},{4,6},{5,7},{6,0},{7,1},{8,10},{9,11},{10,... | collective-permute-start | bytes 98312 | tf_op jit(solution)/shard_map/ppermute | solution.py:24
  41.1 11.3 %collective-permute-start.11 = (f32[3,64,128]{2,1,0:T(8,128)S(1)}, f32[3,64,128]{2,1,0:T(8,128)S(1)}, u32[]{:S(2)}, u32[]{:S(2)}) collective-permute-start(f32[3,64,128]{2,1,0:T(8,128)S(1)} %get-tuple-element.47), channel_id=1, source_target_pairs={{0,4},{1,5},{2,6},{3,7},{4,0},{5,1},{6,2},{7,3},{8,12},{9,13},{10,... | collective-permute-start | bytes 294920 | tf_op jit(solution)/shard_map/ppermute | solution.py:24
  46.7 8.8 %collective-permute-start.10 = (f32[3,64,128]{2,1,0:T(8,128)S(1)}, f32[3,64,128]{2,1,0:T(8,128)S(1)}, u32[]{:S(2)}, u32[]{:S(2)}) collective-permute-start(f32[3,64,128]{2,1,0:T(8,128)S(1)} %get-tuple-element.47), channel_id=1, source_target_pairs={{0,6},{1,7},{2,0},{3,1},{4,2},{5,3},{6,4},{7,5},{8,14},{9,15},{10,... | collective-permute-start | bytes 294920 | tf_op jit(solution)/shard_map/ppermute | solution.py:24
  48.7 85.5 %collective-permute-start.22 = (f32[1024,384]{1,0:T(8,128)S(1)}, f32[1024,384]{1,0:T(8,128)S(1)}, u32[]{:S(2)}, u32[]{:S(2)}) collective-permute-start(f32[1024,384]{1,0:T(8,128)S(1)} %collective-permute-done.21.refs_7_), channel_id=1, source_target_pairs={{0,8},{8,16},{16,24},{24,32},{32,40},{40,48},{48,56},{56,64},{64,7... | collective-permute-start | bytes 4718600 | tf_op jit(solution)/shard_map/ppermute | solution.py:61
  52.5 23.1 %collective-permute-start.7 = (f32[64,128]{1,0:T(8,128)S(1)}, f32[64,128]{1,0:T(8,128)S(1)}, u32[]{:S(2)}, u32[]{:S(2)}) collective-permute-start(f32[64,128]{1,0:T(8,128)S(1)} %get-tuple-element.43), channel_id=1, source_target_pairs={{0,16},{1,17},{2,18},{3,19},{4,20},{5,21},{6,22},{7,23},{8,24},{9,... | collective-permute-start | bytes 98312 | tf_op jit(solution)/shard_map/ppermute | solution.py:24
  55.5 35.4 %collective-permute-start.13 = (f32[4,3,64,128]{3,2,1,0:T(8,128)S(1)}, f32[4,3,64,128]{3,2,1,0:T(8,128)S(1)}, u32[]{:S(2)}, u32[]{:S(2)}) collective-permute-start(f32[4,3,64,128]{3,2,1,0:T(8,128)S(1)} %pad_maximum_fusion.refs_6_), channel_id=1, source_target_pairs={{0,1},{1,0},{2,3},{3,2},{4,5},{5,4},{6,7},{7,6},{8,9},{9,8},{10,11... | collective-permute-start | bytes 1179656 | tf_op jit(solution)/shard_map/ppermute | solution.py:24
  75.6 5.3 %collective-permute-start.6 = (f32[5,64,128]{2,1,0:T(8,128)S(1)}, f32[5,64,128]{2,1,0:T(8,128)S(1)}, u32[]{:S(2)}, u32[]{:S(2)}) collective-permute-start(f32[5,64,128]{2,1,0:T(8,128)S(1)} %get-tuple-element.42.level.refs_0_), channel_id=1, source_target_pairs={{0,24},{1,25},{2,26},{3,27},{4,28},{5,29},{6,30},{7,31},{8,0},{9,1... | collective-permute-start | bytes 491528 | tf_op jit(solution)/shard_map/ppermute | solution.py:24
  80.9 6.5 %collective-permute-start.5 = (f32[5,64,128]{2,1,0:T(8,128)S(1)}, f32[5,64,128]{2,1,0:T(8,128)S(1)}, u32[]{:S(2)}, u32[]{:S(2)}) collective-permute-start(f32[5,64,128]{2,1,0:T(8,128)S(1)} %get-tuple-element.42.level.refs_0_), channel_id=1, source_target_pairs={{0,8},{1,9},{2,10},{3,11},{4,12},{5,13},{6,14},{7,15},{8,16},{9,17... | collective-permute-start | bytes 491528 | tf_op jit(solution)/shard_map/ppermute | solution.py:24
  87.5 8.3 %collective-permute-start.8 = (f32[8,64,128]{2,1,0:T(8,128)S(1)}, f32[8,64,128]{2,1,0:T(8,128)S(1)}, u32[]{:S(2)}, u32[]{:S(2)}) collective-permute-start(f32[8,64,128]{2,1,0:T(8,128)S(1)} %get-tuple-element.45), channel_id=1, source_target_pairs={{0,32},{1,33},{2,34},{3,35},{4,36},{5,37},{6,38},{7,39},{8,40},{9,... | collective-permute-start | bytes 786440 | tf_op jit(solution)/shard_map/ppermute | solution.py:24
  90.9 57.7 %collective-permute-start.18 = (f32[1024,384]{1,0:T(8,128)S(1)}, f32[1024,384]{1,0:T(8,128)S(1)}, u32[]{:S(2)}, u32[]{:S(2)}) collective-permute-start(f32[1024,384]{1,0:T(8,128)S(1)} %get-tuple-element.50), channel_id=1, source_target_pairs={{1,2},{2,1},{3,4},{4,3},{5,6},{6,5},{7,8},{8,7},{9,10},{10,9},{11,... | collective-permute-start | bytes 4718600 | tf_op jit(solution)/shard_map/ppermute | solution.py:48
  95.8 19.5 %collective-permute-start.9 = (f32[8,64,128]{2,1,0:T(8,128)S(1)}, f32[8,64,128]{2,1,0:T(8,128)S(1)}, u32[]{:S(2)}, u32[]{:S(2)}) collective-permute-start(f32[8,64,128]{2,1,0:T(8,128)S(1)} %get-tuple-element.46), channel_id=1, source_target_pairs={{32,0},{33,1},{34,2},{35,3},{36,4},{37,5},{38,6},{39,7},{40,8},{41... | collective-permute-start | bytes 786440 | tf_op jit(solution)/shard_map/ppermute | solution.py:24
  97.7 44.4 %collective-permute-start.20 = (f32[1024,256]{1,0:T(8,128)S(1)}, f32[1024,256]{1,0:T(8,128)S(1)}, u32[]{:S(2)}, u32[]{:S(2)}) collective-permute-start(f32[1024,256]{1,0:T(8,128)S(1)} %collective-permute-done.19.refs_7_), channel_id=1, source_target_pairs={{0,8},{8,16},{16,24},{24,32},{32,40},{40,48},{48,56},{56,64},{64,7... | collective-permute-start | bytes 3145736 | tf_op jit(solution)/shard_map/ppermute | solution.py:61
  117.8 1.4 collective-permute-start.14
  119.2 5.5 %collective-permute-start.15 = (f32[2,64,128]{2,1,0:T(8,128)S(1)}, f32[2,64,128]{2,1,0:T(8,128)S(1)}, u32[]{:S(2)}, u32[]{:S(2)}) collective-permute-start(f32[2,64,128]{2,1,0:T(8,128)S(1)} %get-tuple-element.48), channel_id=1, source_target_pairs={{0,2},{1,7},{2,4},{3,1},{4,6},{5,3},{6,0},{7,5},{8,10},{9,15},{10,... | collective-permute-start | bytes 196616 | tf_op jit(solution)/shard_map/ppermute | solution.py:24
  124.8 7.7 %collective-permute-start.16 = (f32[2,64,128]{2,1,0:T(8,128)S(1)}, f32[2,64,128]{2,1,0:T(8,128)S(1)}, u32[]{:S(2)}, u32[]{:S(2)}) collective-permute-start(f32[2,64,128]{2,1,0:T(8,128)S(1)} %get-tuple-element.49), channel_id=1, source_target_pairs={{0,4},{3,7},{4,0},{7,3},{8,12},{11,15},{12,8},{15,11},{16,20},{19,... | collective-permute-start | bytes 196616 | tf_op jit(solution)/shard_map/ppermute | solution.py:24
  132.5 1.8 %copy-start = (s32[2,3]{1,0:T(2,128)S(1)}, s32[2,3]{1,0:T(2,128)}, u32[]{:S(2)}) copy-start(s32[2,3]{1,0:T(2,128)} %near_list.5) | copy-start | bytes 76
  132.5 1.6 %collective-permute-start.17 = (f32[2,2,64,128]{3,2,1,0:T(8,128)S(1)}, f32[2,2,64,128]{3,2,1,0:T(8,128)S(1)}, u32[]{:S(2)}, u32[]{:S(2)}) collective-permute-start(f32[2,2,64,128]{3,2,1,0:T(8,128)S(1)} %pad_maximum_fusion.1.back), channel_id=1, source_target_pairs={{0,1},{1,0},{2,3},{3,2},{4,5},{5,4},{6,7},{7,6},{8,9},{9,8},{10,11... | collective-permute-start | bytes 393224 | tf_op jit(solution)/shard_map/ppermute | solution.py:24

commit v3 on v2

--- a/solution.py
+++ b/solution.py
@@ -317,6 +317,59 @@
     return small_call(block_kernel, [half, half], near_blocks, scalars=0)
 
 
+def source_of(device, near_list, leaf, m):
+    core = device[0] % 2
+    local = near_list[leaf, m] - 2 * device[0]
+    before = jnp.where(core == 0, 4, 2) + local + 2
+    after = jnp.where(core == 0, 2, 4) + local - 2
+    return jnp.where(local < 0, before, jnp.where(local > 1, after, local))
+
+
+def add_product(buffer, rows, n_high, n_low, both, i, slot, span):
+    terms = dot(n_high[i], both[slot])
+    buffer[rows, :] += terms[:, :span] + (
+        terms[:, span:] + dot(n_low[i], both[slot, :, pl.ds(0, span)])
+    )
+
+
+def early_kernel(at, width, device, near_list, *refs):
+    n_high, n_low, p_high, p_low, chip, wide, table, buffer, both = refs
+    span = width * LANES
+    cols = pl.ds(at * LANES, span)
+    high, low = pl.ds(0, span), pl.ds(span, span)
+    for i in range(2):
+        rows = pl.ds(i * 512, 512)
+        both[i, :, high], both[i, :, low] = p_high[rows, cols], p_low[rows, cols]
+        both[2 + i, :, high], both[2 + i, :, low] = split(chip[rows, cols])
+    for leaf in range(2):
+        rows = pl.ds(leaf * 512, 512)
+        buffer[rows, :] = dot(wide[rows, :], table[:, cols])
+        for m in range(3):
+            slot = source_of(device, near_list, leaf, m)
+
+            @pl.when(slot < 4)
+            def _(leaf=leaf, m=m, rows=rows, slot=slot):
+                add_product(buffer, rows, n_high, n_low, both, leaf * 3 + m, slot, span)
+
+
+def near_early(device, near_list, arrays):
+    at, width = CHUNKS[-1]
+    cols = width * LANES
+    (buffer,) = pl.pallas_call(
+        functools.partial(early_kernel, at, width),
+        out_shape=[shape(1024, cols)],
+        in_specs=[SMEM] * 2 + [VMEM] * len(arrays),
+        out_specs=[VMEM],
+        scratch_shapes=[pltpu.VMEM((4, 512, 2 * cols), jnp.bfloat16)],
+        compiler_params=pltpu.CompilerParams(vmem_limit_bytes=16 << 20),
+        cost_estimate=pl.CostEstimate(
+            flops=1_000_000_000 * width, bytes_accessed=2_000_000, transcendentals=0
+        ),
+        name="near_early",
+    )(device, near_list, *arrays)
+    return buffer
+
+
 def near_kernel(at, width, at_old, last, device, near_list, *refs):
     n_high, n_low, p_high, p_low, chip, wide, table, cross, relay = refs[:9]
     both, sems = refs[-2:]
@@ -331,8 +384,9 @@
     high, low = pl.ds(0, span), pl.ds(span, span)
     for i in range(2):
         rows = pl.ds(i * 512, 512)
-        both[i, :, high], both[i, :, low] = p_high[rows, cols], p_low[rows, cols]
-        both[2 + i, :, high], both[2 + i, :, low] = split(chip[rows, cols])
+        if not last:
+            both[i, :, high], both[i, :, low] = p_high[rows, cols], p_low[rows, cols]
+            both[2 + i, :, high], both[2 + i, :, low] = split(chip[rows, cols])
         beside = cross[rows, :]
         if at < CHUNKS[RINGS][0]:
             beside = jnp.where(z == 3 * core, relay[rows, :], beside)
@@ -348,18 +402,24 @@
         copies[-1].start()
     for leaf in range(2):
         rows = pl.ds(leaf * 512, 512)
-        total = dot(wide[rows, :], table[:, cols])
-        for m in range(3):
-            i = leaf * 3 + m
-            local = near_list[leaf, m] - 2 * device[0]
-            before = jnp.where(core == 0, 4, 2) + local + 2
-            after = jnp.where(core == 0, 2, 4) + local - 2
-            slot = jnp.where(local < 0, before, jnp.where(local > 1, after, local))
-            wide_terms = dot(n_high[i], both[slot])
-            total += wide_terms[:, :span]
-            total += wide_terms[:, span:]
-            total += dot(n_low[i], both[slot, :, high])
-        buffer[rows, :] = total
+        if last:
+            buffer[rows, :] = refs[10][rows, :]
+            for m in range(3):
+                slot = source_of(device, near_list, leaf, m)
+
+                @pl.when(slot >= 4)
+                def _(leaf=leaf, m=m, rows=rows, slot=slot):
+                    add_product(buffer, rows, n_high, n_low, both, leaf * 3 + m, slot, span)
+        else:
+            total = dot(wide[rows, :], table[:, cols])
+            for m in range(3):
+                i = leaf * 3 + m
+                slot = source_of(device, near_list, leaf, m)
+                wide_terms = dot(n_high[i], both[slot])
+                total += wide_terms[:, :span]
+                total += wide_terms[:, span:]
+                total += dot(n_low[i], both[slot, :, high])
+            buffer[rows, :] = total
         if last:
             copies.append(
                 pltpu.make_async_copy(buffer.at[rows], out.at[rows, cols], sems.at[leaf])
@@ -369,7 +429,7 @@
         copy.wait()
 
 
-def near_field(chunk, device, near_list, arrays, old, out):
+def near_field(chunk, device, near_list, arrays, old, early, out):
     (at, width), last = CHUNKS[chunk], chunk == len(CHUNKS) - 1
     cols = width * LANES
     at_old = CHUNKS[chunk - 1][0] if chunk else None
@@ -378,6 +438,9 @@
     aliases = {}
     if chunk:
         args.append(old)
+        in_specs.append(VMEM)
+    if last:
+        args.append(early)
         in_specs.append(VMEM)
     if out is not None:
         in_specs.append(ANY)
@@ -448,12 +511,7 @@
             relays.append(crosses[i])
 
     own_table = jnp.stack(
-        [
-            couplings,
-            along_z(couplings, -1),
-            along_z(couplings, 2),
-            along_z(couplings, 1),
-        ]
+        [couplings, along_z(couplings, -1), along_z(couplings, 2), along_z(couplings, 1)]
     )
     other_table = chip_swap(own_table)
 
@@ -516,10 +574,12 @@
         unpack_kernel, [shape(192, 1024, dtype=jnp.bfloat16)], device, down, other, back, other_back
     )
 
+    local = (*blocks, p_high, p_low, chip, wide, table)
+    early = near_early(device, near_list, local)
     out = old = None
     for i, (cross, relay) in enumerate(zip(crosses, relays)):
         arrays = (*blocks, p_high, p_low, chip, wide, table, cross, relay)
-        out, old = near_field(i, device, near_list, arrays, old, out)
+        out, old = near_field(i, device, near_list, arrays, old, early, out)
     return out
 
 

time: 159 us -> 140 us (0.88)
  waiting for transfers between devices: 89.6 us -> 66.7 us
  Pallas kernels: 32.2 us -> 35.8 us
    ppermute x20, waiting for transfers between devices: 89.6 us -> 66.7 us  [permuted(): return lax.ppermute(shard, 'leaf', pairs)]
    pallas_call x0 -> x1, Pallas kernels: none -> 7.15 us  [near_early(): pl.pallas_call(functools.partial(early_kernel, at, width), out_shape=[sha...]
    pallas_call x3, Pallas kernels: 23 us -> 19.5 us  [near_field(): pl.pallas_call(functools.partial(near_kernel, at, width, at_old, last), o...]
  transfers between devices with their start and end apart: 23 -> 23, of which waited for: 12 -> 13; matrix products, arithmetic and copies ran while one was open for 0% -> 0% of each run, Pallas kernels for 15% -> 22%
where the time goes in v3:
time: 140 us; the launch traced here: 139 us
  waiting for transfers between devices  66.7 us (48%)
  Pallas kernels  35.8 us (26%)
  starting transfers between devices  34.9 us (25%)
    ppermute x20, waiting for transfers between devices, permuted(): return lax.ppermute(shard, 'leaf', pairs)  66.7 us
    ppermute x20, starting transfers between devices, permuted(): return lax.ppermute(shard, 'leaf', pairs)  25.8 us
    pallas_call x3, Pallas kernels, near_field(): pl.pallas_call(functools.partial(near_kernel, at, width, at_old, last), o...  19.5 us
    pallas_call x1, Pallas kernels, near_early(): pl.pallas_call(functools.partial(early_kernel, at, width), out_shape=[sha...  7.15 us
    ppermute x2, starting transfers between devices, relayed(): return lax.ppermute(shard, 'leaf', pairs)  6.69 us
    pallas_call x1, Pallas kernels, leaf_stage(): pl.pallas_call(leaf_kernel, out_shape=shapes, in_specs=[SMEM] * 3 + [HBM]...  5.19 us
    pallas_call x7, Pallas kernels, small_call(): pl.pallas_call(kernel, out_shape=outs, in_specs=[SMEM] * scalars + [VMEM]...  4.01 us
  transfers between devices with their start and end apart: 23, of which 13 were waited for; matrix products, arithmetic and copies ran while one was open for 0% of the time, Pallas kernels for 22%

profile of v3, /device:TPU:2, one launch (start us, length us, event | category | flops | bytes accessed | tf_op | source)
XLA Modules:
  0.0 139.4 jit_solution(5413229494182063034)
XLA Ops:
  0.7 0.8 copy-done.1
  1.5 5.2 %leaf_stage.1 = (f32[64,512]{1,0:T(8,128)S(1)}, f32[64,512]{1,0:T(8,128)S(1)}, f32[3,64,128]{2,1,0:T(8,128)S(1)}, f32[4,64,64]{2,1,0:T(8,128)S(1)}, bf16[1024,19...) custom-call(s32[1]{0:T(128)} %bitcast.device, ...), custom_call_target="tpu_custom_call" | custom-call | flops 400000000 | bytes 8000000 | tf_op jit(solution)/shard_map/leaf_stage/pallas_call | solution.py:166
  6.7 4.2 %collective-permute-start.21 = (f32[1024,384]{1,0:T(8,128)S(1)}, f32[1024,384]{1,0:T(8,128)S(1)}, u32[]{:S(2)}, u32[]{:S(2)}) collective-permute-start(f32[1024,384]{1,0:T(8,128)S(1)} %get-tuple-element.52), channel_id=1, source_target_pairs={{0,7},{1,2},{2,1},{3,4},{4,3},{5,6},{6,5},{7,0},{8,15},{9,10},{10,... | collective-permute-start | bytes 4718600 | tf_op jit(solution)/shard_map/ppermute | solution.py:24
  10.9 0.1 collective-permute-start.19
  11.0 18.0 %collective-permute-done.21.refs_7_ = f32[1024,384]{1,0:T(8,128)S(1)} collective-permute-done((f32[1024,384]{1,0:T(8,128)S(1)}, f32[1024,384]{1,0:T(8,128)S(1)}, u32[]{:S(2)}, u32[]{:S(2)}) %collective-permute-start.21) | collective-permute-done | bytes 1572896 | tf_op jit(solution)/shard_map/ppermute | solution.py:24
  29.0 3.5 %collective-permute-start.22 = (f32[1024,384]{1,0:T(8,128)S(1)}, f32[1024,384]{1,0:T(8,128)S(1)}, u32[]{:S(2)}, u32[]{:S(2)}) collective-permute-start(f32[1024,384]{1,0:T(8,128)S(1)} %collective-permute-done.21.refs_7_), channel_id=1, source_target_pairs={{0,8},{8,16},{16,24},{24,32},{32,40},{40,48},{48,56},{56,64},{64,7... | collective-permute-start | bytes 4718600 | tf_op jit(solution)/shard_map/ppermute | solution.py:61
  32.5 0.1 collective-permute-start.12
  32.6 0.1 shard_map.119
  32.6 3.3 %collective-permute-start.2 = (f32[64,128]{1,0:T(8,128)S(1)}, f32[64,128]{1,0:T(8,128)S(1)}, u32[]{:S(2)}, u32[]{:S(2)}) collective-permute-start(f32[64,128]{1,0:T(8,128)S(1)} %get-tuple-element.38), channel_id=1, source_target_pairs={{0,6},{1,7},{2,0},{3,1},{4,2},{5,3},{6,4},{7,5},{8,14},{9,15},{10,... | collective-permute-start | bytes 98312 | tf_op jit(solution)/shard_map/ppermute | solution.py:24
  35.9 3.5 %collective-permute-done.12 = f32[3,64,128]{2,1,0:T(8,128)S(1)} collective-permute-done((f32[3,64,128]{2,1,0:T(8,128)S(1)}, f32[3,64,128]{2,1,0:T(8,128)S(1)}, u32[]{:S(2)}, u32[]{:S(2)}) %collective-permute-start.12) | collective-permute-done | bytes 98336 | tf_op jit(solution)/shard_map/ppermute | solution.py:24
  39.4 0.0 collective-permute-start.3
  39.4 1.7 %collective-permute-done.2.second = f32[64,128]{1,0:T(8,128)S(1)} collective-permute-done((f32[64,128]{1,0:T(8,128)S(1)}, f32[64,128]{1,0:T(8,128)S(1)}, u32[]{:S(2)}, u32[]{:S(2)}) %collective-permute-start.2) | collective-permute-done | bytes 32800 | tf_op jit(solution)/shard_map/ppermute | solution.py:24
  41.2 3.7 %collective-permute-done.3.third = f32[64,128]{1,0:T(8,128)S(1)} collective-permute-done((f32[64,128]{1,0:T(8,128)S(1)}, f32[64,128]{1,0:T(8,128)S(1)}, u32[]{:S(2)}, u32[]{:S(2)}) %collective-permute-start.3) | collective-permute-done | bytes 32800 | tf_op jit(solution)/shard_map/ppermute | solution.py:24
  44.9 1.4 %collective-permute-start.11 = (f32[3,64,128]{2,1,0:T(8,128)S(1)}, f32[3,64,128]{2,1,0:T(8,128)S(1)}, u32[]{:S(2)}, u32[]{:S(2)}) collective-permute-start(f32[3,64,128]{2,1,0:T(8,128)S(1)} %get-tuple-element.47), channel_id=1, source_target_pairs={{0,4},{1,5},{2,6},{3,7},{4,0},{5,1},{6,2},{7,3},{8,12},{9,13},{10,... | collective-permute-start | bytes 294920 | tf_op jit(solution)/shard_map/ppermute | solution.py:24
  46.3 0.8 collective-permute-done.4.fourth
  47.1 1.7 %collective-permute-start.10 = (f32[3,64,128]{2,1,0:T(8,128)S(1)}, f32[3,64,128]{2,1,0:T(8,128)S(1)}, u32[]{:S(2)}, u32[]{:S(2)}) collective-permute-start(f32[3,64,128]{2,1,0:T(8,128)S(1)} %get-tuple-element.47), channel_id=1, source_target_pairs={{0,6},{1,7},{2,0},{3,1},{4,2},{5,3},{6,4},{7,5},{8,14},{9,15},{10,... | collective-permute-start | bytes 294920 | tf_op jit(solution)/shard_map/ppermute | solution.py:24
  48.7 0.3 shard_map.120
  49.0 2.0 %collective-permute-done.11 = f32[3,64,128]{2,1,0:T(8,128)S(1)} collective-permute-done((f32[3,64,128]{2,1,0:T(8,128)S(1)}, f32[3,64,128]{2,1,0:T(8,128)S(1)}, u32[]{:S(2)}, u32[]{:S(2)}) %collective-permute-start.11) | collective-permute-done | bytes 98336 | tf_op jit(solution)/shard_map/ppermute | solution.py:24
  51.0 2.6 %collective-permute-start.6 = (f32[5,64,128]{2,1,0:T(8,128)S(1)}, f32[5,64,128]{2,1,0:T(8,128)S(1)}, u32[]{:S(2)}, u32[]{:S(2)}) collective-permute-start(f32[5,64,128]{2,1,0:T(8,128)S(1)} %get-tuple-element.42.level.refs_0_), channel_id=1, source_target_pairs={{0,24},{1,25},{2,26},{3,27},{4,28},{5,29},{6,30},{7,31},{8,0},{9,1... | collective-permute-start | bytes 491528 | tf_op jit(solution)/shard_map/ppermute | solution.py:24
  53.6 2.3 %collective-permute-start.7 = (f32[64,128]{1,0:T(8,128)S(1)}, f32[64,128]{1,0:T(8,128)S(1)}, u32[]{:S(2)}, u32[]{:S(2)}) collective-permute-start(f32[64,128]{1,0:T(8,128)S(1)} %get-tuple-element.43), channel_id=1, source_target_pairs={{0,16},{1,17},{2,18},{3,19},{4,20},{5,21},{6,22},{7,23},{8,24},{9,... | collective-permute-start | bytes 98312 | tf_op jit(solution)/shard_map/ppermute | solution.py:24
  55.9 3.1 %collective-permute-done.7.across = f32[64,128]{1,0:T(8,128)S(1)} collective-permute-done((f32[64,128]{1,0:T(8,128)S(1)}, f32[64,128]{1,0:T(8,128)S(1)}, u32[]{:S(2)}, u32[]{:S(2)}) %collective-permute-start.7) | collective-permute-done | bytes 32800 | tf_op jit(solution)/shard_map/ppermute | solution.py:24
  59.0 0.0 collective-permute-done.6.above.refs_2_
  59.0 2.0 %collective-permute-start.5 = (f32[5,64,128]{2,1,0:T(8,128)S(1)}, f32[5,64,128]{2,1,0:T(8,128)S(1)}, u32[]{:S(2)}, u32[]{:S(2)}) collective-permute-start(f32[5,64,128]{2,1,0:T(8,128)S(1)} %get-tuple-element.42.level.refs_0_), channel_id=1, source_target_pairs={{0,8},{1,9},{2,10},{3,11},{4,12},{5,13},{6,14},{7,15},{8,16},{9,17... | collective-permute-start | bytes 491528 | tf_op jit(solution)/shard_map/ppermute | solution.py:24
  61.0 5.9 %collective-permute-done.5.below.refs_1_ = f32[5,64,128]{2,1,0:T(8,128)S(1)} collective-permute-done((f32[5,64,128]{2,1,0:T(8,128)S(1)}, f32[5,64,128]{2,1,0:T(8,128)S(1)}, u32[]{:S(2)}, u32[]{:S(2)}) %collective-permute-start.5) | collective-permute-done | bytes 163872 | tf_op jit(solution)/shard_map/ppermute | solution.py:24
  66.9 3.3 %collective-permute-start.8 = (f32[8,64,128]{2,1,0:T(8,128)S(1)}, f32[8,64,128]{2,1,0:T(8,128)S(1)}, u32[]{:S(2)}, u32[]{:S(2)}) collective-permute-start(f32[8,64,128]{2,1,0:T(8,128)S(1)} %get-tuple-element.45), channel_id=1, source_target_pairs={{0,32},{1,33},{2,34},{3,35},{4,36},{5,37},{6,38},{7,39},{8,40},{9,... | collective-permute-start | bytes 786440 | tf_op jit(solution)/shard_map/ppermute | solution.py:24
  70.3 2.5 %collective-permute-start.9 = (f32[8,64,128]{2,1,0:T(8,128)S(1)}, f32[8,64,128]{2,1,0:T(8,128)S(1)}, u32[]{:S(2)}, u32[]{:S(2)}) collective-permute-start(f32[8,64,128]{2,1,0:T(8,128)S(1)} %get-tuple-element.46), channel_id=1, source_target_pairs={{32,0},{33,1},{34,2},{35,3},{36,4},{37,5},{38,6},{39,7},{40,8},{41... | collective-permute-start | bytes 786440 | tf_op jit(solution)/shard_map/ppermute | solution.py:24
  72.8 3.7 %collective-permute-done.8.refs_4_ = f32[8,64,128]{2,1,0:T(8,128)S(1)} collective-permute-done((f32[8,64,128]{2,1,0:T(8,128)S(1)}, f32[8,64,128]{2,1,0:T(8,128)S(1)}, u32[]{:S(2)}, u32[]{:S(2)}) %collective-permute-start.8) | collective-permute-done | bytes 262176 | tf_op jit(solution)/shard_map/ppermute | solution.py:24
  76.5 2.4 %collective-permute-start.18 = (f32[1024,384]{1,0:T(8,128)S(1)}, f32[1024,384]{1,0:T(8,128)S(1)}, u32[]{:S(2)}, u32[]{:S(2)}) collective-permute-start(f32[1024,384]{1,0:T(8,128)S(1)} %get-tuple-element.50), channel_id=1, source_target_pairs={{1,2},{2,1},{3,4},{4,3},{5,6},{6,5},{7,8},{8,7},{9,10},{10,9},{11,... | collective-permute-start | bytes 4718600 | tf_op jit(solution)/shard_map/ppermute | solution.py:48
  78.9 3.2 %collective-permute-start.20 = (f32[1024,256]{1,0:T(8,128)S(1)}, f32[1024,256]{1,0:T(8,128)S(1)}, u32[]{:S(2)}, u32[]{:S(2)}) collective-permute-start(f32[1024,256]{1,0:T(8,128)S(1)} %collective-permute-done.19.refs_7_), channel_id=1, source_target_pairs={{0,8},{8,16},{16,24},{24,32},{32,40},{40,48},{48,56},{56,64},{64,7... | collective-permute-start | bytes 3145736 | tf_op jit(solution)/shard_map/ppermute | solution.py:61
  82.1 0.0 collective-permute-done.9.refs_5_
  82.2 2.6 %shard_map.122.down = f32[4,64,128]{2,1,0:T(8,128)S(1)} custom-call(s32[1]{0:T(128)} %bitcast.device, s32[64]{0:T(128)S(1)} %copy-done.2, s32[16]{0:T(128)S(1)} %copy-done.3, f32[5,64,128]{2,1,0:T(8,128)S(1)} %get-tuple-element.42.level.refs_0_, f32[5,64,128]{2,1,0:T(8,128)S(1)} %collective-permute-done.5.below.refs_1_, ...), custom_call_target="tpu_custom_call" | custom-call | flops 10000000 | bytes 1000000 | tf_op jit(solution)/shard_map/pallas_call | solution.py:193
  84.7 0.1 collective-permute-start.14
  84.8 1.3 collective-permute-done.14.other
  86.2 0.1 collective-permute-start.15
  86.3 16.8 %collective-permute-done.15 = f32[2,64,128]{2,1,0:T(8,128)S(1)} collective-permute-done((f32[2,64,128]{2,1,0:T(8,128)S(1)}, f32[2,64,128]{2,1,0:T(8,128)S(1)}, u32[]{:S(2)}, u32[]{:S(2)}) %collective-permute-start.15) | collective-permute-done | bytes 65568 | tf_op jit(solution)/shard_map/ppermute | solution.py:24
  103.1 1.9 %collective-permute-start.16 = (f32[2,64,128]{2,1,0:T(8,128)S(1)}, f32[2,64,128]{2,1,0:T(8,128)S(1)}, u32[]{:S(2)}, u32[]{:S(2)}) collective-permute-start(f32[2,64,128]{2,1,0:T(8,128)S(1)} %get-tuple-element.49), channel_id=1, source_target_pairs={{0,4},{3,7},{4,0},{7,3},{8,12},{11,15},{12,8},{15,11},{16,20},{19,... | collective-permute-start | bytes 196616 | tf_op jit(solution)/shard_map/ppermute | solution.py:24
  105.0 5.7 %collective-permute-done.16 = f32[2,64,128]{2,1,0:T(8,128)S(1)} collective-permute-done((f32[2,64,128]{2,1,0:T(8,128)S(1)}, f32[2,64,128]{2,1,0:T(8,128)S(1)}, u32[]{:S(2)}, u32[]{:S(2)}) %collective-permute-start.16) | collective-permute-done | bytes 65568 | tf_op jit(solution)/shard_map/ppermute | solution.py:24
  110.8 0.0 copy-start
  110.8 0.3 collective-permute-start.17
  111.1 1.0 shard_map.118
  112.0 0.3 collective-permute-done.17.other_back
  112.4 0.1 shard_map.124.refs_6_
  112.5 0.0 collective-permute-done.22.refs_8_
  112.5 0.0 collective-permute-done.refs_4_
  112.5 7.9 %near_field.3.refs_9_ = f32[1024,384]{1,0:T(8,128)S(1)} custom-call(s32[1]{0:T(128)} %bitcast.device, s32[2,3]{1,0:T(2,128)S(1)} %copy-done, bf16[6,512,512]{2,1,0:T(8,128)(2,1)S(1)} %get-tuple-element.30.refs_0_, bf16[6,512,512]{2,1,0:T(8,128)(2,1)S(1)} %get-tuple-element.31.refs_1_, bf16[1024,1024]{1,0:T(8,128)(2,1)S(1)} %get-tuple-element.32.refs_2_, ...), custom_call_target="tpu_custom_call" | custom-call | flops 3750000128 | bytes 2000000 | tf_op jit(solution)/shard_map/near_field/pallas_call | solution.py:461
  120.4 6.4 %near_field.4 = (f32[1024,1024]{1,0:T(8,128)}, f32[1024,256]{1,0:T(8,128)S(1)}) custom-call(s32[1]{0:T(128)} %bitcast.device, s32[2,3]{1,0:T(2,128)S(1)} %copy-done, bf16[6,512,512]{2,1,0:T(8,128)(2,1)S(1)} %get-tuple-element.30.refs_0_, bf16[6,512,512]{2,1,0:T(8,128)(2,1)S(1)} %get-tuple-element.31.refs_1_, ...), custom_call_target="tpu_custom_call" | custom-call | flops 2500000000 | bytes 2000000 | tf_op jit(solution)/shard_map/near_field/pallas_call | solution.py:461
  126.9 7.2 %near_early.1.refs_10_ = f32[1024,384]{1,0:T(8,128)S(1)} custom-call(s32[1]{0:T(128)} %bitcast.device, s32[2,3]{1,0:T(2,128)S(1)} %copy-done, bf16[6,512,512]{2,1,0:T(8,128)(2,1)S(1)} %get-tuple-element.30.refs_0_, bf16[6,512,512]{2,1,0:T(8,128)(2,1)S(1)} %get-tuple-element.31.refs_1_, bf16[1024,1024]{1,0:T(8,128)(2,1)S(1)} %get-tuple-element.32.refs_2_, ...), custom_call_target="tpu_custom_call" | custom-call | flops 3000000000 | bytes 2000000 | tf_op jit(solution)/shard_map/near_early/pallas_call | solution.py:358
  134.0 5.2 %near_field.5 = f32[1024,1024]{1,0:T(8,128)} custom-call(s32[1]{0:T(128)} %bitcast.device, s32[2,3]{1,0:T(2,128)S(1)} %copy-done, bf16[6,512,512]{2,1,0:T(8,128)(2,1)S(1)} %get-tuple-element.30.refs_0_, bf16[6,512,512]{2,1,0:T(8,128)(2,1)S(1)} %get-tuple-element.31.refs_1_, ...), custom_call_target="tpu_custom_call", output_to_operand_aliasing={{}: (13, {})} | custom-call | flops 3750000128 | bytes 2000000 | tf_op jit(solution)/shard_map/near_field/pallas_call | solution.py:461
  (25 shorter events, 0.1 us)
Async XLA Ops:
  0.0 112.5 %collective-permute-start = (f32[1024,1024]{1,0:T(8,128)}, f32[1024,1024]{1,0:T(8,128)}, u32[]{:S(2)}, u32[]{:S(2)}) collective-permute-start(f32[1024,1024]{1,0:T(8,128)} %probes.1), channel_id=1, source_target_pairs={{0,1},{1,0},{2,3},{3,2},{4,5},{5,4},{6,7},{7,6},{8,9},{9,8},{10,11... | collective-permute-start | bytes 12582920 | tf_op jit(solution)/shard_map/ppermute | solution.py:24
  0.7 110.4 %slice-start = ((s8[6291456]{0:T(1024)(128)(4,1)}), s8[4194304]{0:T(1024)(128)(4,1)S(1)}, s32[]{:S(2)}) async-start(s8[6291456]{0:T(1024)(128)(4,1)} %bitcast.8), calls=%async_computation | async-start | bytes 8388608
  0.7 0.8 copy-start.1
  1.5 80.7 %copy-start.2 = (s32[64]{0:T(128)S(1)}, s32[64]{0:T(128)}, u32[]{:S(2)}) copy-start(s32[64]{0:T(128)} %count_one.1) | copy-start | bytes 772
  1.5 80.7 %copy-start.3 = (s32[16]{0:T(128)S(1)}, s32[16]{0:T(128)}, u32[]{:S(2)}) copy-start(s32[16]{0:T(128)} %count_two.1) | copy-start | bytes 196
  1.5 109.6 %slice-start.1 = ((s8[6291456]{0:T(1024)(128)(4,1)}), s8[2097152]{0:T(1024)(128)(4,1)S(1)}, s32[]{:S(2)}) async-start(s8[6291456]{0:T(1024)(128)(4,1)} %bitcast.8), calls=%async_computation.1 | async-start | bytes 4194304
  6.7 22.3 %collective-permute-start.21 = (f32[1024,384]{1,0:T(8,128)S(1)}, f32[1024,384]{1,0:T(8,128)S(1)}, u32[]{:S(2)}, u32[]{:S(2)}) collective-permute-start(f32[1024,384]{1,0:T(8,128)S(1)} %get-tuple-element.52), channel_id=1, source_target_pairs={{0,7},{1,2},{2,1},{3,4},{4,3},{5,6},{6,5},{7,0},{8,15},{9,10},{10,... | collective-permute-start | bytes 4718600 | tf_op jit(solution)/shard_map/ppermute | solution.py:24
  10.9 68.0 %collective-permute-start.19 = (f32[1024,256]{1,0:T(8,128)S(1)}, f32[1024,256]{1,0:T(8,128)S(1)}, u32[]{:S(2)}, u32[]{:S(2)}) collective-permute-start(f32[1024,256]{1,0:T(8,128)S(1)} %get-tuple-element.51), channel_id=1, source_target_pairs={{0,7},{1,2},{2,1},{3,4},{4,3},{5,6},{6,5},{7,0},{8,15},{9,10},{10,... | collective-permute-start | bytes 3145736 | tf_op jit(solution)/shard_map/ppermute | solution.py:24
  11.0 21.6 %collective-permute-start.1 = (f32[64,512]{1,0:T(8,128)S(1)}, f32[64,512]{1,0:T(8,128)S(1)}, u32[]{:S(2)}, u32[]{:S(2)}) collective-permute-start(f32[64,512]{1,0:T(8,128)S(1)} %get-tuple-element.36), channel_id=1, source_target_pairs={{0,1},{1,0},{2,3},{3,2},{4,5},{5,4},{6,7},{7,6},{8,9},{9,8},{10,11... | collective-permute-start | bytes 393224 | tf_op jit(solution)/shard_map/ppermute | solution.py:24
  29.0 83.5 %collective-permute-start.22 = (f32[1024,384]{1,0:T(8,128)S(1)}, f32[1024,384]{1,0:T(8,128)S(1)}, u32[]{:S(2)}, u32[]{:S(2)}) collective-permute-start(f32[1024,384]{1,0:T(8,128)S(1)} %collective-permute-done.21.refs_7_), channel_id=1, source_target_pairs={{0,8},{8,16},{16,24},{24,32},{32,40},{40,48},{48,56},{56,64},{64,7... | collective-permute-start | bytes 4718600 | tf_op jit(solution)/shard_map/ppermute | solution.py:61
  32.5 6.9 %collective-permute-start.12 = (f32[3,64,128]{2,1,0:T(8,128)S(1)}, f32[3,64,128]{2,1,0:T(8,128)S(1)}, u32[]{:S(2)}, u32[]{:S(2)}) collective-permute-start(f32[3,64,128]{2,1,0:T(8,128)S(1)} %get-tuple-element.47), channel_id=1, source_target_pairs={{0,2},{1,3},{2,4},{3,5},{4,6},{5,7},{6,0},{7,1},{8,10},{9,11},{10,... | collective-permute-start | bytes 294920 | tf_op jit(solution)/shard_map/ppermute | solution.py:24
  32.6 8.5 %collective-permute-start.2 = (f32[64,128]{1,0:T(8,128)S(1)}, f32[64,128]{1,0:T(8,128)S(1)}, u32[]{:S(2)}, u32[]{:S(2)}) collective-permute-start(f32[64,128]{1,0:T(8,128)S(1)} %get-tuple-element.38), channel_id=1, source_target_pairs={{0,6},{1,7},{2,0},{3,1},{4,2},{5,3},{6,4},{7,5},{8,14},{9,15},{10,... | collective-permute-start | bytes 98312 | tf_op jit(solution)/shard_map/ppermute | solution.py:24
  39.4 5.4 %collective-permute-start.3 = (f32[64,128]{1,0:T(8,128)S(1)}, f32[64,128]{1,0:T(8,128)S(1)}, u32[]{:S(2)}, u32[]{:S(2)}) collective-permute-start(f32[64,128]{1,0:T(8,128)S(1)} %get-tuple-element.39), channel_id=1, source_target_pairs={{0,4},{1,5},{2,6},{3,7},{4,0},{5,1},{6,2},{7,3},{8,12},{9,13},{10,... | collective-permute-start | bytes 98312 | tf_op jit(solution)/shard_map/ppermute | solution.py:24
  41.2 5.9 %collective-permute-start.4 = (f32[64,128]{1,0:T(8,128)S(1)}, f32[64,128]{1,0:T(8,128)S(1)}, u32[]{:S(2)}, u32[]{:S(2)}) collective-permute-start(f32[64,128]{1,0:T(8,128)S(1)} %get-tuple-element.40), channel_id=1, source_target_pairs={{0,2},{1,3},{2,4},{3,5},{4,6},{5,7},{6,0},{7,1},{8,10},{9,11},{10,... | collective-permute-start | bytes 98312 | tf_op jit(solution)/shard_map/ppermute | solution.py:24
  44.9 6.1 %collective-permute-start.11 = (f32[3,64,128]{2,1,0:T(8,128)S(1)}, f32[3,64,128]{2,1,0:T(8,128)S(1)}, u32[]{:S(2)}, u32[]{:S(2)}) collective-permute-start(f32[3,64,128]{2,1,0:T(8,128)S(1)} %get-tuple-element.47), channel_id=1, source_target_pairs={{0,4},{1,5},{2,6},{3,7},{4,0},{5,1},{6,2},{7,3},{8,12},{9,13},{10,... | collective-permute-start | bytes 294920 | tf_op jit(solution)/shard_map/ppermute | solution.py:24
  47.1 6.5 %collective-permute-start.10 = (f32[3,64,128]{2,1,0:T(8,128)S(1)}, f32[3,64,128]{2,1,0:T(8,128)S(1)}, u32[]{:S(2)}, u32[]{:S(2)}) collective-permute-start(f32[3,64,128]{2,1,0:T(8,128)S(1)} %get-tuple-element.47), channel_id=1, source_target_pairs={{0,6},{1,7},{2,0},{3,1},{4,2},{5,3},{6,4},{7,5},{8,14},{9,15},{10,... | collective-permute-start | bytes 294920 | tf_op jit(solution)/shard_map/ppermute | solution.py:24
  51.0 8.0 %collective-permute-start.6 = (f32[5,64,128]{2,1,0:T(8,128)S(1)}, f32[5,64,128]{2,1,0:T(8,128)S(1)}, u32[]{:S(2)}, u32[]{:S(2)}) collective-permute-start(f32[5,64,128]{2,1,0:T(8,128)S(1)} %get-tuple-element.42.level.refs_0_), channel_id=1, source_target_pairs={{0,24},{1,25},{2,26},{3,27},{4,28},{5,29},{6,30},{7,31},{8,0},{9,1... | collective-permute-start | bytes 491528 | tf_op jit(solution)/shard_map/ppermute | solution.py:24
  53.6 5.4 %collective-permute-start.7 = (f32[64,128]{1,0:T(8,128)S(1)}, f32[64,128]{1,0:T(8,128)S(1)}, u32[]{:S(2)}, u32[]{:S(2)}) collective-permute-start(f32[64,128]{1,0:T(8,128)S(1)} %get-tuple-element.43), channel_id=1, source_target_pairs={{0,16},{1,17},{2,18},{3,19},{4,20},{5,21},{6,22},{7,23},{8,24},{9,... | collective-permute-start | bytes 98312 | tf_op jit(solution)/shard_map/ppermute | solution.py:24
  59.0 11.3 %collective-permute-start.13 = (f32[4,3,64,128]{3,2,1,0:T(8,128)S(1)}, f32[4,3,64,128]{3,2,1,0:T(8,128)S(1)}, u32[]{:S(2)}, u32[]{:S(2)}) collective-permute-start(f32[4,3,64,128]{3,2,1,0:T(8,128)S(1)} %pad_maximum_fusion.refs_6_), channel_id=1, source_target_pairs={{0,1},{1,0},{2,3},{3,2},{4,5},{5,4},{6,7},{7,6},{8,9},{9,8},{10,11... | collective-permute-start | bytes 1179656 | tf_op jit(solution)/shard_map/ppermute | solution.py:24
  59.0 7.9 %collective-permute-start.5 = (f32[5,64,128]{2,1,0:T(8,128)S(1)}, f32[5,64,128]{2,1,0:T(8,128)S(1)}, u32[]{:S(2)}, u32[]{:S(2)}) collective-permute-start(f32[5,64,128]{2,1,0:T(8,128)S(1)} %get-tuple-element.42.level.refs_0_), channel_id=1, source_target_pairs={{0,8},{1,9},{2,10},{3,11},{4,12},{5,13},{6,14},{7,15},{8,16},{9,17... | collective-permute-start | bytes 491528 | tf_op jit(solution)/shard_map/ppermute | solution.py:24
  66.9 9.6 %collective-permute-start.8 = (f32[8,64,128]{2,1,0:T(8,128)S(1)}, f32[8,64,128]{2,1,0:T(8,128)S(1)}, u32[]{:S(2)}, u32[]{:S(2)}) collective-permute-start(f32[8,64,128]{2,1,0:T(8,128)S(1)} %get-tuple-element.45), channel_id=1, source_target_pairs={{0,32},{1,33},{2,34},{3,35},{4,36},{5,37},{6,38},{7,39},{8,40},{9,... | collective-permute-start | bytes 786440 | tf_op jit(solution)/shard_map/ppermute | solution.py:24
  70.3 11.9 %collective-permute-start.9 = (f32[8,64,128]{2,1,0:T(8,128)S(1)}, f32[8,64,128]{2,1,0:T(8,128)S(1)}, u32[]{:S(2)}, u32[]{:S(2)}) collective-permute-start(f32[8,64,128]{2,1,0:T(8,128)S(1)} %get-tuple-element.46), channel_id=1, source_target_pairs={{32,0},{33,1},{34,2},{35,3},{36,4},{37,5},{38,6},{39,7},{40,8},{41... | collective-permute-start | bytes 786440 | tf_op jit(solution)/shard_map/ppermute | solution.py:24
  76.5 57.6 %collective-permute-start.18 = (f32[1024,384]{1,0:T(8,128)S(1)}, f32[1024,384]{1,0:T(8,128)S(1)}, u32[]{:S(2)}, u32[]{:S(2)}) collective-permute-start(f32[1024,384]{1,0:T(8,128)S(1)} %get-tuple-element.50), channel_id=1, source_target_pairs={{1,2},{2,1},{3,4},{4,3},{5,6},{6,5},{7,8},{8,7},{9,10},{10,9},{11,... | collective-permute-start | bytes 4718600 | tf_op jit(solution)/shard_map/ppermute | solution.py:48
  78.9 41.5 %collective-permute-start.20 = (f32[1024,256]{1,0:T(8,128)S(1)}, f32[1024,256]{1,0:T(8,128)S(1)}, u32[]{:S(2)}, u32[]{:S(2)}) collective-permute-start(f32[1024,256]{1,0:T(8,128)S(1)} %collective-permute-done.19.refs_7_), channel_id=1, source_target_pairs={{0,8},{8,16},{16,24},{24,32},{32,40},{40,48},{48,56},{56,64},{64,7... | collective-permute-start | bytes 3145736 | tf_op jit(solution)/shard_map/ppermute | solution.py:61
  84.7 1.4 %collective-permute-start.14 = (f32[4,64,128]{2,1,0:T(8,128)S(1)}, f32[4,64,128]{2,1,0:T(8,128)S(1)}, u32[]{:S(2)}, u32[]{:S(2)}) collective-permute-start(f32[4,64,128]{2,1,0:T(8,128)S(1)} %shard_map.122.down), channel_id=1, source_target_pairs={{0,1},{1,0},{2,3},{3,2},{4,5},{5,4},{6,7},{7,6},{8,9},{9,8},{10,11... | collective-permute-start | bytes 393224 | tf_op jit(solution)/shard_map/ppermute | solution.py:24
  86.2 16.9 %collective-permute-start.15 = (f32[2,64,128]{2,1,0:T(8,128)S(1)}, f32[2,64,128]{2,1,0:T(8,128)S(1)}, u32[]{:S(2)}, u32[]{:S(2)}) collective-permute-start(f32[2,64,128]{2,1,0:T(8,128)S(1)} %get-tuple-element.48), channel_id=1, source_target_pairs={{0,2},{1,7},{2,4},{3,1},{4,6},{5,3},{6,0},{7,5},{8,10},{9,15},{10,... | collective-permute-start | bytes 196616 | tf_op jit(solution)/shard_map/ppermute | solution.py:24
  103.1 7.7 %collective-permute-start.16 = (f32[2,64,128]{2,1,0:T(8,128)S(1)}, f32[2,64,128]{2,1,0:T(8,128)S(1)}, u32[]{:S(2)}, u32[]{:S(2)}) collective-permute-start(f32[2,64,128]{2,1,0:T(8,128)S(1)} %get-tuple-element.49), channel_id=1, source_target_pairs={{0,4},{3,7},{4,0},{7,3},{8,12},{11,15},{12,8},{15,11},{16,20},{19,... | collective-permute-start | bytes 196616 | tf_op jit(solution)/shard_map/ppermute | solution.py:24
  110.8 1.8 %copy-start = (s32[2,3]{1,0:T(2,128)S(1)}, s32[2,3]{1,0:T(2,128)}, u32[]{:S(2)}) copy-start(s32[2,3]{1,0:T(2,128)} %near_list.7) | copy-start | bytes 76
  110.8 1.6 %collective-permute-start.17 = (f32[2,2,64,128]{3,2,1,0:T(8,128)S(1)}, f32[2,2,64,128]{3,2,1,0:T(8,128)S(1)}, u32[]{:S(2)}, u32[]{:S(2)}) collective-permute-start(f32[2,2,64,128]{3,2,1,0:T(8,128)S(1)} %pad_maximum_fusion.1.back), channel_id=1, source_target_pairs={{0,1},{1,0},{2,3},{3,2},{4,5},{5,4},{6,7},{7,6},{8,9},{9,8},{10,11... | collective-permute-start | bytes 393224 | tf_op jit(solution)/shard_map/ppermute | solution.py:24
